TPU v7x, 1024 devices: a whole 8x8x8 slice. The times are simulated.
1024 devices in a mesh: gx: 8 (over x), gy: 8 (over y), gz: 16 (over z, core).
Axes of the slice: x: 8, y: 8, z: 8, core: 2. Of those that a mesh axis runs over, the one named last changes fastest.
Arguments:
- loads: float32 [8, 8, 16, 12, 768], P('gx', 'gy', 'gz')
- dual_ops: bfloat16 [8, 8, 16, 768, 768], P('gx', 'gy', 'gz'), as said below
- precond: bfloat16 [8, 8, 16, 768, 768], P('gx', 'gy', 'gz'), as said below
- counts: int32 [8, 8, 16, 18], P('gx', 'gy', 'gz'), may hold values from 0 to 96, as said below
- signs: int32 [8, 8, 16, 768], P('gx', 'gy', 'gz'), may hold values from -1 to 1, as said below
Outputs:
- multipliers: float32 [8, 8, 16, 12, 768], P('gx', 'gy', 'gz')
- residual: float32 [8, 8, 16, 12, 768], P('gx', 'gy', 'gz')
Inputs may be any that keep to these rules, and one draw needn't show every extreme that they name: counts[s, d] equals counts[s + offset(d), opp(d)] and is 0 where s + offset(d) lies outside the grid; inside, a face block holds 48 to 96 live multipliers and an edge block 8 to 16, and both bounds 96 and 16 are reached; live slots are the first ones of their block. `signs`: every entry is -1 or 1. `dual_ops`: each subdomain's matrix is symmetric and positive definite. `precond`: each subdomain's matrix is symmetric and positive definite.
All inputs are finite; a program needn't handle non-finite values.
Results may differ from a plain program's by a relative error of at most 0.0055.
The roundings to bfloat16 on the way count: a program that leaves them out, or rounds other values in their place, can miss the bound.
Values sent between devices are 32-bit elements; how exact they have to be, the bound alone decides.
No kernel may reach another device: no remote copies, remote signals or barrier semaphores. Data moves between devices by JAX's collectives and lax.ppermute only.
A program may use at most 32 MiB of HBM per device.

v0:
```python
import jax
import jax.numpy as jnp
import numpy as np
from jax import lax
from jax.sharding import PartitionSpec as P

FACE = 96
EDGE = 16
ITERS = 2


DIRECTIONS = (
    (1, 0, 0),
    (-1, 0, 0),
    (0, 1, 0),
    (0, -1, 0),
    (0, 0, 1),
    (0, 0, -1),
    (1, 1, 0),
    (1, -1, 0),
    (-1, 1, 0),
    (-1, -1, 0),
    (1, 0, 1),
    (1, 0, -1),
    (-1, 0, 1),
    (-1, 0, -1),
    (0, 1, 1),
    (0, 1, -1),
    (0, -1, 1),
    (0, -1, -1),
)


def extended(cells, sides, width):
    for axis, dim in sides:
        count = lax.axis_size(axis)
        ends = count - 1
        head = lax.slice_in_dim(cells, 0, width, axis=dim)
        tail = lax.slice_in_dim(cells, cells.shape[dim] - width, cells.shape[dim], axis=dim)
        cells = jnp.concatenate(
            [
                lax.ppermute(tail, axis, [(i, (i + 1) % count) for i in range(ends)]),
                cells,
                lax.ppermute(head, axis, [((i + 1) % count, i) for i in range(ends)]),
            ],
            axis=dim,
        )
    return cells


def opposite(course):
    heading = DIRECTIONS[course]
    return DIRECTIONS.index((-heading[0], -heading[1], -heading[2]))


def block_table():
    capacity = [FACE] * 6 + [EDGE] * 12
    offsets = [sum(capacity[:course]) for course in range(18)]
    return (capacity, offsets)


def global_sum(values):
    return lax.psum(values, ("gx", "gy", "gz"))


def per_device(loads, dual_ops, precond, counts, signs):
    capacity, offsets = block_table()
    order_max = sum(capacity)
    owners = np.zeros((18, order_max), np.int32)
    position = np.zeros((order_max,), np.int32)
    for course in range(18):
        owners[course, offsets[course] : offsets[course] + capacity[course]] = 1
        position[offsets[course] : offsets[course] + capacity[course]] = np.arange(capacity[course])
    limits = jnp.sum(counts[0, 0, 0][:, None] * jnp.asarray(owners, jnp.int32), axis=0)
    alive = (jnp.asarray(position, jnp.int32) < limits).astype(jnp.float32)
    signed = signs[0, 0, 0].astype(jnp.float32) * alive

    def neighbours(contribution):
        beside_all = extended(contribution[None, None, None], (("gx", 0), ("gy", 1), ("gz", 2)), 1)
        pieces = []
        for course, heading in enumerate(DIRECTIONS):
            back = opposite(course)
            nearby = beside_all[1 + heading[0], 1 + heading[1], 1 + heading[2]]
            pieces.append(nearby[:, offsets[back] : offsets[back] + capacity[back]])
        return jnp.concatenate(pieces, axis=1)

    def assemble(contribution):
        return alive * (contribution + neighbours(contribution))

    def apply_and_dot(matrix, vector):
        scaled = (signed * vector).astype(jnp.bfloat16)
        contribution = signed * jnp.dot(scaled, matrix, preferred_element_type=jnp.float32)
        whole = assemble(contribution)
        product = global_sum(0.5 * jnp.sum(vector * whole, axis=1))
        return (whole, product)

    dual_matrix = dual_ops[0, 0, 0]
    pre_matrix = precond[0, 0, 0]
    residual = assemble(alive * loads[0, 0, 0])
    multipliers = jnp.zeros_like(residual)
    direction = residual
    gamma_old = None
    for iteration in range(ITERS):
        smoothed, gamma_new = apply_and_dot(pre_matrix, residual)
        if iteration == 0:
            direction = smoothed
        else:
            direction = smoothed + (gamma_new / gamma_old)[:, None] * direction
        image, curvature = apply_and_dot(dual_matrix, direction)
        step_size = gamma_new / curvature
        multipliers = multipliers + step_size[:, None] * direction
        residual = residual - step_size[:, None] * image
        gamma_old = gamma_new
    return (multipliers[None, None, None], residual[None, None, None])


def solution(mesh):
    placed = (
        P("gx", "gy", "gz", None, None),
        P("gx", "gy", "gz", None, None),
        P("gx", "gy", "gz", None, None),
        P("gx", "gy", "gz", None),
        P("gx", "gy", "gz", None),
    )
    return jax.shard_map(
        per_device,
        mesh=mesh,
        in_specs=placed,
        out_specs=(P("gx", "gy", "gz", None, None), P("gx", "gy", "gz", None, None)),
        check_vma=False,
    )
```

profile of v0, /device:TPU:1, one launch (start us, length us, event | category | flops | bytes accessed | tf_op | source)
XLA Modules:
  0.0 529.0 jit_solution(5356411821846021304)
XLA Ops:
  3.9 3.9 collective-permute-start.1
  7.8 1.3 collective-permute-start
  9.1 3.5 collective-permute-done
  12.7 3.3 collective-permute-start.3
  16.0 1.3 collective-permute-start.2
  18.1 3.8 collective-permute-done.2
  21.9 8.3 %collective-permute-start.5 = (f32[3,3,1,12,768]{4,3,2,1,0:T(8,128)S(1)}, f32[3,3,1,12,768]{4,3,2,1,0:T(8,128)S(1)}, u32[]{:S(2)}, u32[]{:S(2)}) collective-permute-start(f32[3,3,1,12,768]{4,3,2,1,0:T(8,128)S(1)} %pad_maximum_fusion), channel_id=1, source_target_pairs={{0,1},{1,2},{2,3},{3,4},{4,5},{5,6},{6,7},{7,8},{8,9},{9,10},{10,1... | collective-permute-start | bytes 995336 | tf_op jit(solution)/shard_map/ppermute | solution.py:42
  30.3 6.6 %collective-permute-start.4 = (f32[3,3,1,12,768]{4,3,2,1,0:T(8,128)S(1)}, f32[3,3,1,12,768]{4,3,2,1,0:T(8,128)S(1)}, u32[]{:S(2)}, u32[]{:S(2)}) collective-permute-start(f32[3,3,1,12,768]{4,3,2,1,0:T(8,128)S(1)} %pad_maximum_fusion), channel_id=1, source_target_pairs={{1,0},{2,1},{3,2},{4,3},{5,4},{6,5},{7,6},{8,7},{9,8},{10,9},{11,1... | collective-permute-start | bytes 995336 | tf_op jit(solution)/shard_map/ppermute | solution.py:44
  37.4 2.5 collective-permute-done.4
  40.6 3.1 collective-permute-start.7
  43.7 1.3 collective-permute-start.6
  45.0 4.0 collective-permute-done.6
  49.0 3.6 collective-permute-start.9
  54.7 4.9 collective-permute-done.8
  59.7 3.7 collective-permute-start.11
  63.4 1.9 collective-permute-start.10
  65.8 2.8 collective-permute-done.11
  68.9 4.2 collective-permute-done.10
  73.8 5.1 collective-permute-start.13
  80.3 4.1 collective-permute-done.12
  84.4 5.2 collective-permute-start.15
  89.6 1.3 collective-permute-start.14
  91.7 4.4 collective-permute-done.14
  96.1 3.6 collective-permute-start.17
  99.7 1.9 collective-permute-start.16
  102.1 2.8 collective-permute-done.17
  105.1 4.2 collective-permute-done.16
  109.9 121.2 %all-reduce = (f32[12]{0:T(128)S(1)}, f32[12]{0:T(128)S(1)}) all-reduce(f32[12]{0:T(128)S(1)} %broadcast_multiply_fusion.3, f32[12]{0:T(128)S(1)} %broadcast_multiply_fusion.2), channel_id=1, replica_groups=mesh['gx'=8,'gy'=8,'gz'=16] {'gx','gy','gz'}, use_global_device_ids=true, to_apply=%region_2.0 | all-reduce | flops 24 | bytes 192 | tf_op jit(solution)/shard_map/psum | solution.py:63
  231.5 2.9 collective-permute-start.19
  234.4 1.3 collective-permute-start.18
  235.7 3.5 collective-permute-done.18
  239.3 2.9 collective-permute-start.21
  244.3 3.8 collective-permute-done.20
  248.1 6.0 %collective-permute-start.23 = (f32[3,3,1,12,768]{4,3,2,1,0:T(8,128)S(1)}, f32[3,3,1,12,768]{4,3,2,1,0:T(8,128)S(1)}, u32[]{:S(2)}, u32[]{:S(2)}) collective-permute-start(f32[3,3,1,12,768]{4,3,2,1,0:T(8,128)S(1)} %pad_maximum_fusion.3), channel_id=1, source_target_pairs={{0,1},{1,2},{2,3},{3,4},{4,5},{5,6},{6,7},{7,8},{8,9},{9,10},{10,1... | collective-permute-start | bytes 995336 | tf_op jit(solution)/shard_map/ppermute | solution.py:42
  254.2 1.9 collective-permute-start.22
  256.6 2.8 collective-permute-done.23
  259.6 4.2 collective-permute-done.22
  264.4 114.6 %psum.30 = f32[12]{0:T(128)S(1)} all-reduce(f32[12]{0:T(128)S(1)} %broadcast_multiply_fusion.1), channel_id=1, replica_groups=mesh['gx'=8,'gy'=8,'gz'=16] {'gx','gy','gz'}, use_global_device_ids=true, to_apply=%region_6.0 | all-reduce | flops 12 | bytes 96 | tf_op jit(solution)/shard_map/psum | solution.py:63
  379.4 1.9 collective-permute-start.25
  382.6 4.6 collective-permute-done.24
  387.1 3.4 collective-permute-start.27
  390.5 1.3 collective-permute-start.26
  392.6 3.8 collective-permute-done.26
  396.4 5.0 collective-permute-start.29
  401.5 1.9 collective-permute-start.28
  403.9 2.8 collective-permute-done.29
  407.0 4.2 collective-permute-done.28
  411.7 115.9 %psum.31 = f32[12]{0:T(128)S(1)} all-reduce(f32[12]{0:T(128)S(1)} %broadcast_multiply_fusion), channel_id=1, replica_groups=mesh['gx'=8,'gy'=8,'gz'=16] {'gx','gy','gz'}, use_global_device_ids=true, to_apply=%region_8.0 | all-reduce | flops 12 | bytes 96 | tf_op jit(solution)/shard_map/psum | solution.py:63
  (164 shorter events, 21.1 us)
Async XLA Ops:
  0.6 39.6 %copy-start = (bf16[1,1,1,768,768]{4,3,2,1,0:T(8,128)(2,1)S(1)}, bf16[1,1,1,768,768]{4,3,2,1,0:T(8,128)(2,1)}, u32[]{:S(2)}) copy-start(bf16[1,1,1,768,768]{4,3,2,1,0:T(8,128)(2,1)} %param.9) | copy-start | bytes 3538948
  3.9 5.2 collective-permute-start.1
  7.8 4.8 collective-permute-start
  12.7 5.4 %collective-permute-start.3 = (f32[3,1,1,12,768]{4,3,2,1,0:T(8,128)S(1)}, f32[3,1,1,12,768]{4,3,2,1,0:T(8,128)S(1)}, u32[]{:S(2)}, u32[]{:S(2)}) collective-permute-start(f32[3,1,1,12,768]{4,3,2,1,0:T(8,128)S(1)} %pad_maximum_fusion.5), channel_id=1, source_target_pairs={{0,16},{16,32},{32,48},{48,64},{64,80},{80,96},{96,112},{1,17},{17... | collective-permute-start | bytes 331784 | tf_op jit(solution)/shard_map/ppermute | solution.py:42
  16.0 5.9 %collective-permute-start.2 = (f32[3,1,1,12,768]{4,3,2,1,0:T(8,128)S(1)}, f32[3,1,1,12,768]{4,3,2,1,0:T(8,128)S(1)}, u32[]{:S(2)}, u32[]{:S(2)}) collective-permute-start(f32[3,1,1,12,768]{4,3,2,1,0:T(8,128)S(1)} %pad_maximum_fusion.5), channel_id=1, source_target_pairs={{16,0},{32,16},{48,32},{64,48},{80,64},{96,80},{112,96},{17,1},{33... | collective-permute-start | bytes 331784 | tf_op jit(solution)/shard_map/ppermute | solution.py:44
  21.9 18.3 %copy-start.2 = (f32[1,1,1,12,768]{4,2,3,1,0:T(1,128)S(1)}, f32[1,1,1,12,768]{4,2,3,1,0:T(1,128)}, u32[]{:S(2)}) copy-start(f32[1,1,1,12,768]{4,2,3,1,0:T(1,128)} %param.7) | copy-start | bytes 110596
  21.9 15.2 %collective-permute-start.5 = (f32[3,3,1,12,768]{4,3,2,1,0:T(8,128)S(1)}, f32[3,3,1,12,768]{4,3,2,1,0:T(8,128)S(1)}, u32[]{:S(2)}, u32[]{:S(2)}) collective-permute-start(f32[3,3,1,12,768]{4,3,2,1,0:T(8,128)S(1)} %pad_maximum_fusion), channel_id=1, source_target_pairs={{0,1},{1,2},{2,3},{3,4},{4,5},{5,6},{6,7},{7,8},{8,9},{9,10},{10,1... | collective-permute-start | bytes 995336 | tf_op jit(solution)/shard_map/ppermute | solution.py:42
  30.3 9.6 %collective-permute-start.4 = (f32[3,3,1,12,768]{4,3,2,1,0:T(8,128)S(1)}, f32[3,3,1,12,768]{4,3,2,1,0:T(8,128)S(1)}, u32[]{:S(2)}, u32[]{:S(2)}) collective-permute-start(f32[3,3,1,12,768]{4,3,2,1,0:T(8,128)S(1)} %pad_maximum_fusion), channel_id=1, source_target_pairs={{1,0},{2,1},{3,2},{4,3},{5,4},{6,5},{7,6},{8,7},{9,8},{10,9},{11,1... | collective-permute-start | bytes 995336 | tf_op jit(solution)/shard_map/ppermute | solution.py:44
  40.6 4.4 collective-permute-start.7
  43.7 5.3 collective-permute-start.6
  49.0 5.7 %collective-permute-start.9 = (f32[3,1,1,12,768]{4,3,2,1,0:T(8,128)S(1)}, f32[3,1,1,12,768]{4,3,2,1,0:T(8,128)S(1)}, u32[]{:S(2)}, u32[]{:S(2)}) collective-permute-start(f32[3,1,1,12,768]{4,3,2,1,0:T(8,128)S(1)} %pad_maximum_fusion.6), channel_id=1, source_target_pairs={{0,16},{16,32},{32,48},{48,64},{64,80},{80,96},{96,112},{1,17},{17... | collective-permute-start | bytes 331784 | tf_op jit(solution)/shard_map/ppermute | solution.py:42
  52.6 7.0 %collective-permute-start.8 = (f32[3,1,1,12,768]{4,3,2,1,0:T(8,128)S(1)}, f32[3,1,1,12,768]{4,3,2,1,0:T(8,128)S(1)}, u32[]{:S(2)}, u32[]{:S(2)}) collective-permute-start(f32[3,1,1,12,768]{4,3,2,1,0:T(8,128)S(1)} %pad_maximum_fusion.6), channel_id=1, source_target_pairs={{16,0},{32,16},{48,32},{64,48},{80,64},{96,80},{112,96},{17,1},{33... | collective-permute-start | bytes 331784 | tf_op jit(solution)/shard_map/ppermute | solution.py:44
  59.7 13.9 %copy-start.1 = (bf16[1,1,1,768,768]{4,3,2,1,0:T(8,128)(2,1)S(1)}, bf16[1,1,1,768,768]{4,3,2,1,0:T(8,128)(2,1)}, u32[]{:S(2)}) copy-start(bf16[1,1,1,768,768]{4,3,2,1,0:T(8,128)(2,1)} %param.8) | copy-start | bytes 3538948
  59.7 9.0 %collective-permute-start.11 = (f32[3,3,1,12,768]{4,3,2,1,0:T(8,128)S(1)}, f32[3,3,1,12,768]{4,3,2,1,0:T(8,128)S(1)}, u32[]{:S(2)}, u32[]{:S(2)}) collective-permute-start(f32[3,3,1,12,768]{4,3,2,1,0:T(8,128)S(1)} %pad_maximum_fusion.1), channel_id=1, source_target_pairs={{0,1},{1,2},{2,3},{3,4},{4,5},{5,6},{6,7},{7,8},{8,9},{9,10},{10,1... | collective-permute-start | bytes 995336 | tf_op jit(solution)/shard_map/ppermute | solution.py:42
  63.4 9.6 %collective-permute-start.10 = (f32[3,3,1,12,768]{4,3,2,1,0:T(8,128)S(1)}, f32[3,3,1,12,768]{4,3,2,1,0:T(8,128)S(1)}, u32[]{:S(2)}, u32[]{:S(2)}) collective-permute-start(f32[3,3,1,12,768]{4,3,2,1,0:T(8,128)S(1)} %pad_maximum_fusion.1), channel_id=1, source_target_pairs={{1,0},{2,1},{3,2},{4,3},{5,4},{6,5},{7,6},{8,7},{9,8},{10,9},{11,1... | collective-permute-start | bytes 995336 | tf_op jit(solution)/shard_map/ppermute | solution.py:44
  73.8 6.5 %collective-permute-start.13 = (f32[1,1,1,12,768]{4,3,2,1,0:T(8,128)S(1)}, f32[1,1,1,12,768]{4,3,2,1,0:T(8,128)S(1)}, u32[]{:S(2)}, u32[]{:S(2)}) collective-permute-start(f32[1,1,1,12,768]{4,3,2,1,0:T(8,128)S(1)} %bitcast.256), channel_id=1, source_target_pairs={{0,128},{128,256},{256,384},{384,512},{512,640},{640,768},{768,896... | collective-permute-start | bytes 110600 | tf_op jit(solution)/shard_map/ppermute | solution.py:42
  79.0 5.4 %collective-permute-start.12 = (f32[1,1,1,12,768]{4,3,2,1,0:T(8,128)S(1)}, f32[1,1,1,12,768]{4,3,2,1,0:T(8,128)S(1)}, u32[]{:S(2)}, u32[]{:S(2)}) collective-permute-start(f32[1,1,1,12,768]{4,3,2,1,0:T(8,128)S(1)} %bitcast.257), channel_id=1, source_target_pairs={{128,0},{256,128},{384,256},{512,384},{640,512},{768,640},{896,768... | collective-permute-start | bytes 110600 | tf_op jit(solution)/shard_map/ppermute | solution.py:44
  84.4 7.2 %collective-permute-start.15 = (f32[3,1,1,12,768]{4,3,2,1,0:T(8,128)S(1)}, f32[3,1,1,12,768]{4,3,2,1,0:T(8,128)S(1)}, u32[]{:S(2)}, u32[]{:S(2)}) collective-permute-start(f32[3,1,1,12,768]{4,3,2,1,0:T(8,128)S(1)} %pad_maximum_fusion.7), channel_id=1, source_target_pairs={{0,16},{16,32},{32,48},{48,64},{64,80},{80,96},{96,112},{1,17},{17... | collective-permute-start | bytes 331784 | tf_op jit(solution)/shard_map/ppermute | solution.py:42
  89.6 6.4 %collective-permute-start.14 = (f32[3,1,1,12,768]{4,3,2,1,0:T(8,128)S(1)}, f32[3,1,1,12,768]{4,3,2,1,0:T(8,128)S(1)}, u32[]{:S(2)}, u32[]{:S(2)}) collective-permute-start(f32[3,1,1,12,768]{4,3,2,1,0:T(8,128)S(1)} %pad_maximum_fusion.7), channel_id=1, source_target_pairs={{16,0},{32,16},{48,32},{64,48},{80,64},{96,80},{112,96},{17,1},{33... | collective-permute-start | bytes 331784 | tf_op jit(solution)/shard_map/ppermute | solution.py:44
  96.1 8.8 %collective-permute-start.17 = (f32[3,3,1,12,768]{4,3,2,1,0:T(8,128)S(1)}, f32[3,3,1,12,768]{4,3,2,1,0:T(8,128)S(1)}, u32[]{:S(2)}, u32[]{:S(2)}) collective-permute-start(f32[3,3,1,12,768]{4,3,2,1,0:T(8,128)S(1)} %pad_maximum_fusion.2), channel_id=1, source_target_pairs={{0,1},{1,2},{2,3},{3,4},{4,5},{5,6},{6,7},{7,8},{8,9},{9,10},{10,1... | collective-permute-start | bytes 995336 | tf_op jit(solution)/shard_map/ppermute | solution.py:42
  99.7 9.6 %collective-permute-start.16 = (f32[3,3,1,12,768]{4,3,2,1,0:T(8,128)S(1)}, f32[3,3,1,12,768]{4,3,2,1,0:T(8,128)S(1)}, u32[]{:S(2)}, u32[]{:S(2)}) collective-permute-start(f32[3,3,1,12,768]{4,3,2,1,0:T(8,128)S(1)} %pad_maximum_fusion.2), channel_id=1, source_target_pairs={{1,0},{2,1},{3,2},{4,3},{5,4},{6,5},{7,6},{8,7},{9,8},{10,9},{11,1... | collective-permute-start | bytes 995336 | tf_op jit(solution)/shard_map/ppermute | solution.py:44
  231.5 4.3 collective-permute-start.19
  234.4 4.8 collective-permute-start.18
  239.3 5.0 collective-permute-start.21
  242.2 5.9 %collective-permute-start.20 = (f32[3,1,1,12,768]{4,3,2,1,0:T(8,128)S(1)}, f32[3,1,1,12,768]{4,3,2,1,0:T(8,128)S(1)}, u32[]{:S(2)}, u32[]{:S(2)}) collective-permute-start(f32[3,1,1,12,768]{4,3,2,1,0:T(8,128)S(1)} %pad_maximum_fusion.8), channel_id=1, source_target_pairs={{16,0},{32,16},{48,32},{64,48},{80,64},{96,80},{112,96},{17,1},{33... | collective-permute-start | bytes 331784 | tf_op jit(solution)/shard_map/ppermute | solution.py:44
  248.1 11.3 %collective-permute-start.23 = (f32[3,3,1,12,768]{4,3,2,1,0:T(8,128)S(1)}, f32[3,3,1,12,768]{4,3,2,1,0:T(8,128)S(1)}, u32[]{:S(2)}, u32[]{:S(2)}) collective-permute-start(f32[3,3,1,12,768]{4,3,2,1,0:T(8,128)S(1)} %pad_maximum_fusion.3), channel_id=1, source_target_pairs={{0,1},{1,2},{2,3},{3,4},{4,5},{5,6},{6,7},{7,8},{8,9},{9,10},{10,1... | collective-permute-start | bytes 995336 | tf_op jit(solution)/shard_map/ppermute | solution.py:42
  254.2 9.6 %collective-permute-start.22 = (f32[3,3,1,12,768]{4,3,2,1,0:T(8,128)S(1)}, f32[3,3,1,12,768]{4,3,2,1,0:T(8,128)S(1)}, u32[]{:S(2)}, u32[]{:S(2)}) collective-permute-start(f32[3,3,1,12,768]{4,3,2,1,0:T(8,128)S(1)} %pad_maximum_fusion.3), channel_id=1, source_target_pairs={{1,0},{2,1},{3,2},{4,3},{5,4},{6,5},{7,6},{8,7},{9,8},{10,9},{11,1... | collective-permute-start | bytes 995336 | tf_op jit(solution)/shard_map/ppermute | solution.py:44
  379.4 3.2 collective-permute-start.25
  381.2 5.9 %collective-permute-start.24 = (f32[1,1,1,12,768]{4,3,2,1,0:T(8,128)S(1)}, f32[1,1,1,12,768]{4,3,2,1,0:T(8,128)S(1)}, u32[]{:S(2)}, u32[]{:S(2)}) collective-permute-start(f32[1,1,1,12,768]{4,3,2,1,0:T(8,128)S(1)} %bitcast.253), channel_id=1, source_target_pairs={{128,0},{256,128},{384,256},{512,384},{640,512},{768,640},{896,768... | collective-permute-start | bytes 110600 | tf_op jit(solution)/shard_map/ppermute | solution.py:44
  387.1 5.5 %collective-permute-start.27 = (f32[3,1,1,12,768]{4,3,2,1,0:T(8,128)S(1)}, f32[3,1,1,12,768]{4,3,2,1,0:T(8,128)S(1)}, u32[]{:S(2)}, u32[]{:S(2)}) collective-permute-start(f32[3,1,1,12,768]{4,3,2,1,0:T(8,128)S(1)} %pad_maximum_fusion.9), channel_id=1, source_target_pairs={{0,16},{16,32},{32,48},{48,64},{64,80},{80,96},{96,112},{1,17},{17... | collective-permute-start | bytes 331784 | tf_op jit(solution)/shard_map/ppermute | solution.py:42
  390.5 5.9 %collective-permute-start.26 = (f32[3,1,1,12,768]{4,3,2,1,0:T(8,128)S(1)}, f32[3,1,1,12,768]{4,3,2,1,0:T(8,128)S(1)}, u32[]{:S(2)}, u32[]{:S(2)}) collective-permute-start(f32[3,1,1,12,768]{4,3,2,1,0:T(8,128)S(1)} %pad_maximum_fusion.9), channel_id=1, source_target_pairs={{16,0},{32,16},{48,32},{64,48},{80,64},{96,80},{112,96},{17,1},{33... | collective-permute-start | bytes 331784 | tf_op jit(solution)/shard_map/ppermute | solution.py:44
  396.4 10.3 %collective-permute-start.29 = (f32[3,3,1,12,768]{4,3,2,1,0:T(8,128)S(1)}, f32[3,3,1,12,768]{4,3,2,1,0:T(8,128)S(1)}, u32[]{:S(2)}, u32[]{:S(2)}) collective-permute-start(f32[3,3,1,12,768]{4,3,2,1,0:T(8,128)S(1)} %pad_maximum_fusion.4), channel_id=1, source_target_pairs={{0,1},{1,2},{2,3},{3,4},{4,5},{5,6},{6,7},{7,8},{8,9},{9,10},{10,1... | collective-permute-start | bytes 995336 | tf_op jit(solution)/shard_map/ppermute | solution.py:42
  401.5 9.6 %collective-permute-start.28 = (f32[3,3,1,12,768]{4,3,2,1,0:T(8,128)S(1)}, f32[3,3,1,12,768]{4,3,2,1,0:T(8,128)S(1)}, u32[]{:S(2)}, u32[]{:S(2)}) collective-permute-start(f32[3,3,1,12,768]{4,3,2,1,0:T(8,128)S(1)} %pad_maximum_fusion.4), channel_id=1, source_target_pairs={{1,0},{2,1},{3,2},{4,3},{5,4},{6,5},{7,6},{8,7},{9,8},{10,9},{11,1... | collective-permute-start | bytes 995336 | tf_op jit(solution)/shard_map/ppermute | solution.py:44
where the time goes:
time: 530 us; the launch traced here: 529 us
  blocking collectives  352 us (66%)
  starting transfers between devices  89.4 us (17%)
  waiting for transfers between devices  74.2 us (14%)
  local copies, waits for them, and re-layouts  7.31 us (1%)
    psum x3, blocking collectives, global_sum(): return lax.psum(values, ('gx', 'gy', 'gz'))  352 us
    ppermute x15, starting transfers between devices, extended(): lax.ppermute(tail, axis, [(i, (i + 1) % count) for i in range(ends)])  62.1 us
    ppermute x15, waiting for transfers between devices, extended(): lax.ppermute(head, axis, [((i + 1) % count, i) for i in range(ends)])  59.6 us
    ppermute x15, starting transfers between devices, extended(): lax.ppermute(head, axis, [((i + 1) % count, i) for i in range(ends)])  27.2 us
    ppermute x15, waiting for transfers between devices, extended(): lax.ppermute(tail, axis, [(i, (i + 1) % count) for i in range(ends)])  14.6 us
  transfers between devices with their start and end apart: 30, of which 24 were waited for; matrix products, arithmetic and copies ran while one was open for 1% of the time, Pallas kernels for 0%

commit v1 on v0

v1 whole, which is shorter than its diff:
```python
import jax
import jax.numpy as jnp
import numpy as np
from jax import lax
from jax.sharding import PartitionSpec as P

FACE = 96
EDGE = 16
ITERS = 2


DIRECTIONS = (
    (1, 0, 0),
    (-1, 0, 0),
    (0, 1, 0),
    (0, -1, 0),
    (0, 0, 1),
    (0, 0, -1),
    (1, 1, 0),
    (1, -1, 0),
    (-1, 1, 0),
    (-1, -1, 0),
    (1, 0, 1),
    (1, 0, -1),
    (-1, 0, 1),
    (-1, 0, -1),
    (0, 1, 1),
    (0, 1, -1),
    (0, -1, 1),
    (0, -1, -1),
)


def block_table():
    capacity = [FACE] * 6 + [EDGE] * 12
    offsets = [sum(capacity[:course]) for course in range(18)]
    return (capacity, offsets)


CAPACITY, OFFSETS = block_table()


def block(values, *heading):
    course = DIRECTIONS.index(heading)
    return values[:, OFFSETS[course] : OFFSETS[course] + CAPACITY[course]]


THIRD = 42


def pack(face, edge_a, edge_b, edge_c, edge_d, sums):
    top = jnp.concatenate([face, edge_a, edge_b], axis=1)
    rest = jnp.concatenate([edge_c, edge_d, *sums], axis=1)
    rest = jnp.pad(rest, ((0, 0), (0, THIRD - rest.shape[1])))
    low = jnp.concatenate([rest[0:4], rest[4:8], rest[8:12]], axis=1)
    low = jnp.pad(low, ((0, 0), (0, 128 - 3 * THIRD)))
    return jnp.concatenate([top, low], axis=0)


def unfold(low):
    return jnp.concatenate([low[:, THIRD * i : THIRD * (i + 1)] for i in range(3)], axis=0)


def unpack(tile):
    rest = unfold(tile[12:16])
    return (
        tile[:12, :FACE],
        tile[:12, FACE : FACE + EDGE],
        tile[:12, FACE + EDGE : FACE + 2 * EDGE],
        rest[:, :EDGE],
        rest[:, EDGE : 2 * EDGE],
    )


def shift_swap(axis, ahead, behind):
    ends = lax.axis_size(axis) - 1
    before = lax.ppermute(ahead, axis, [(i, i + 1) for i in range(ends)])
    after = lax.ppermute(behind, axis, [(i + 1, i) for i in range(ends)])
    return before, after


def pair_swap(axis, ahead, behind):
    count = lax.axis_size(axis)
    even = lax.axis_index(axis) % 2 == 0
    inner = [(i, i ^ 1) for i in range(count)]
    outer = [(i, i + 1 if i % 2 else i - 1) for i in range(1, count - 1)]
    near = lax.ppermute(jnp.where(even, ahead, behind), axis, inner)
    far = lax.ppermute(jnp.where(even, behind, ahead), axis, outer)
    return jnp.where(even, far, near), jnp.where(even, near, far)


def line_swap(axis, ahead, behind):
    count = lax.axis_size(axis)
    place = lax.axis_index(axis)
    target = lax.broadcasted_iota(jnp.int32, (count, 1, 1), 0)
    sent = jnp.where(target > place, ahead[None], behind[None])
    got = lax.all_to_all(sent, axis, 0, 0, tiled=True)
    before = lax.dynamic_index_in_dim(got, jnp.maximum(place - 1, 0), 0, keepdims=False)
    after = lax.dynamic_index_in_dim(got, jnp.minimum(place + 1, count - 1), 0, keepdims=False)
    return before, after, jnp.sum(got[:, 12:16, :], axis=0)


def exchange(y, sums=()):
    swaps = (shift_swap, shift_swap, pair_swap)

    def swap(stage, axis, ahead, behind):
        nonlocal sums
        ahead = pack(*ahead, sums)
        behind = pack(*behind, sums)
        if not sums:
            before, after = swaps[stage](axis, ahead, behind)
        else:
            before, after, low = line_swap(axis, ahead, behind)
            rest = unfold(low)
            sums = [rest[:, 2 * EDGE + i : 2 * EDGE + i + 1] for i in range(len(sums))]
        return unpack(before), unpack(after)

    mx, px = swap(
        0,
        "gx",
        (block(y, 1, 0, 0), block(y, 1, 1, 0), block(y, 1, -1, 0), block(y, 1, 0, 1), block(y, 1, 0, -1)),
        (block(y, -1, 0, 0), block(y, -1, 1, 0), block(y, -1, -1, 0), block(y, -1, 0, 1), block(y, -1, 0, -1)),
    )
    my, py = swap(
        1,
        "gy",
        (block(y, 0, 1, 0), mx[1], px[1], block(y, 0, 1, 1), block(y, 0, 1, -1)),
        (block(y, 0, -1, 0), mx[2], px[2], block(y, 0, -1, 1), block(y, 0, -1, -1)),
    )
    mz, pz = swap(
        2,
        "gz",
        (block(y, 0, 0, 1), mx[3], px[3], my[3], py[3]),
        (block(y, 0, 0, -1), mx[4], px[4], my[4], py[4]),
    )
    pieces = [
        px[0], mx[0], py[0], my[0], pz[0], mz[0],
        py[2], my[2], py[1], my[1],
        pz[2], mz[2], pz[1], mz[1],
        pz[4], mz[4], pz[3], mz[3],
    ]
    return jnp.concatenate(pieces, axis=1), sums


def per_device(loads, dual_ops, precond, counts, signs):
    order_max = sum(CAPACITY)
    owners = np.zeros((18, order_max), np.int32)
    position = np.zeros((order_max,), np.int32)
    for course in range(18):
        owners[course, OFFSETS[course] : OFFSETS[course] + CAPACITY[course]] = 1
        position[OFFSETS[course] : OFFSETS[course] + CAPACITY[course]] = np.arange(CAPACITY[course])
    limits = jnp.sum(counts[0, 0, 0][:, None] * jnp.asarray(owners, jnp.int32), axis=0)
    alive = (jnp.asarray(position, jnp.int32) < limits).astype(jnp.float32)
    signed = signs[0, 0, 0].astype(jnp.float32) * alive

    def local(matrix, vector):
        scaled = (signed * vector).astype(jnp.bfloat16)
        return signed * jnp.dot(scaled, matrix, preferred_element_type=jnp.float32)

    def dot(left, right):
        return jnp.sum(left * right, axis=1, keepdims=True)

    def assemble(contribution, sums=()):
        beside, sums = exchange(contribution, sums)
        return alive * (contribution + beside), sums

    dual_matrix = dual_ops[0, 0, 0]
    pre_matrix = precond[0, 0, 0]
    residual, _ = assemble(alive * loads[0, 0, 0])
    part = local(pre_matrix, residual)
    gamma_part = dot(residual, part)
    direction, _ = assemble(part)
    part = local(dual_matrix, direction)
    image, (gamma, curvature) = assemble(part, (gamma_part, dot(direction, part)))
    step = gamma / curvature
    multipliers = step * direction
    residual = residual - step * image
    for _ in range(1, ITERS):
        gamma_old = gamma
        part = local(pre_matrix, residual)
        smoothed, (gamma,) = assemble(part, (dot(residual, part),))
        direction = smoothed + (gamma / gamma_old) * direction
        part = local(dual_matrix, direction)
        image, (curvature,) = assemble(part, (dot(direction, part),))
        step = gamma / curvature
        multipliers = multipliers + step * direction
        residual = residual - step * image
    return (multipliers[None, None, None], residual[None, None, None])


def solution(mesh):
    placed = (
        P("gx", "gy", "gz", None, None),
        P("gx", "gy", "gz", None, None),
        P("gx", "gy", "gz", None, None),
        P("gx", "gy", "gz", None),
        P("gx", "gy", "gz", None),
    )
    return jax.shard_map(
        per_device,
        mesh=mesh,
        in_specs=placed,
        out_specs=(P("gx", "gy", "gz", None, None), P("gx", "gy", "gz", None, None)),
        check_vma=False,
    )
```

time: 530 us -> 203 us (0.38)
  blocking collectives: 352 us -> 20.5 us
  waiting for transfers between devices: 74.2 us -> 57.5 us
  other arithmetic: 4.14 us -> 15.3 us
  starting transfers between devices: 89.4 us -> 94.9 us
    psum x3 -> x0, blocking collectives: 352 us -> none  [global_sum(): return lax.psum(values, ('gx', 'gy', 'gz'))]
    ppermute x30 -> x12, waiting for transfers between devices: 74.2 us -> 2.87 us  [the longest x4 1.55 us: shift_swap(): before = lax.ppermute(ahead, axis, [(i, i + 1) for i in range(ends)])]
    all_to_all x0 -> x7, waiting for transfers between devices: none -> 54.6 us  [line_swap(): got = lax.all_to_all(sent, axis, 0, 0, tiled=True)]
    all_to_all x0 -> x7, starting transfers between devices: none -> 49.2 us  [line_swap(): got = lax.all_to_all(sent, axis, 0, 0, tiled=True)]
    ppermute x30 -> x12, starting transfers between devices: 89.4 us -> 45.7 us  [the longest x4 17.8 us: shift_swap(): before = lax.ppermute(ahead, axis, [(i, i + 1) for i in range(ends)])]
    all_to_all x0 -> x2, blocking collectives: none -> 20.5 us  [line_swap(): got = lax.all_to_all(sent, axis, 0, 0, tiled=True)]
    select_n x0 -> x15, other arithmetic: none -> 5.33 us  [the longest x9 5.15 us: line_swap(): sent = jnp.where(target > place, ahead[None], behind[None])]
  transfers between devices with their start and end apart: 30 -> 19, of which waited for: 24 -> 14; matrix products, arithmetic and copies ran while one was open for 1% -> 2% of each run, Pallas kernels for 0% -> 0%
where the time goes in v1:
time: 203 us; the launch traced here: 202 us
  starting transfers between devices  94.9 us (47%)
  waiting for transfers between devices  57.5 us (28%)
  blocking collectives  20.5 us (10%)
  other arithmetic  15.3 us (8%)
  local copies, waits for them, and re-layouts  10.7 us (5%)
    all_to_all x7, waiting for transfers between devices, line_swap(): got = lax.all_to_all(sent, axis, 0, 0, tiled=True)  54.6 us
    all_to_all x7, starting transfers between devices, line_swap(): got = lax.all_to_all(sent, axis, 0, 0, tiled=True)  49.2 us
    all_to_all x2, blocking collectives, line_swap(): got = lax.all_to_all(sent, axis, 0, 0, tiled=True)  20.5 us
    ppermute x4, starting transfers between devices, shift_swap(): before = lax.ppermute(ahead, axis, [(i, i + 1) for i in range(ends)])  17.8 us
    ppermute x2, starting transfers between devices, pair_swap(): near = lax.ppermute(jnp.where(even, ahead, behind), axis, inner)  13.1 us
    ppermute x2, starting transfers between devices, pair_swap(): far = lax.ppermute(jnp.where(even, behind, ahead), axis, outer)  9.69 us
    select_n x9, other arithmetic, line_swap(): sent = jnp.where(target > place, ahead[None], behind[None])  5.15 us
    ppermute x4, starting transfers between devices, shift_swap(): after = lax.ppermute(behind, axis, [(i + 1, i) for i in range(ends)])  5.14 us
  transfers between devices with their start and end apart: 19, of which 14 were waited for; matrix products, arithmetic and copies ran while one was open for 2% of the time, Pallas kernels for 0%

profile of v1, /device:TPU:1, one launch (start us, length us, event | category | flops | bytes accessed | tf_op | source)
XLA Modules:
  0.0 201.6 jit_solution(11709862024246823204)
XLA Ops:
  0.7 0.8 convert_reduce_fusion
  1.5 1.0 multiply_reduce_fusion
  2.5 0.7 broadcast_select_fusion.17
  3.2 0.8 fusion.24
  4.3 1.3 collective-permute-start
  5.8 4.6 %collective-permute-start.1 = (f32[16,128]{1,0:T(8,128)S(1)}, f32[16,128]{1,0:T(8,128)S(1)}, u32[]{:S(2)}, u32[]{:S(2)}) collective-permute-start(f32[16,128]{1,0:T(8,128)S(1)} %pad_maximum_fusion.5), channel_id=1, source_target_pairs={{0,128},{128,256},{256,384},{384,512},{512,640},{640,768},{768,896... | collective-permute-start | bytes 24584 | tf_op jit(solution)/shard_map/ppermute | solution.py:77
  10.6 0.5 collective-permute-done.1
  11.3 1.3 collective-permute-start.2
  12.6 4.2 %collective-permute-start.3 = (f32[16,128]{1,0:T(8,128)S(1)}, f32[16,128]{1,0:T(8,128)S(1)}, u32[]{:S(2)}, u32[]{:S(2)}) collective-permute-start(f32[16,128]{1,0:T(8,128)S(1)} %pad_maximum_fusion.7), channel_id=1, source_target_pairs={{0,16},{16,32},{32,48},{48,64},{64,80},{80,96},{96,112},{1,17},{17... | collective-permute-start | bytes 24584 | tf_op jit(solution)/shard_map/ppermute | solution.py:77
  18.1 7.8 %collective-permute-start.5 = (f32[16,128]{1,0:T(8,128)S(1)}, f32[16,128]{1,0:T(8,128)S(1)}, u32[]{:S(2)}, u32[]{:S(2)}) collective-permute-start(f32[16,128]{1,0:T(8,128)S(1)} %get-tuple-element.15), channel_id=1, source_target_pairs={{1,2},{2,1},{3,4},{4,3},{5,6},{6,5},{7,8},{8,7},{9,10},{10,9},{11,... | collective-permute-start | bytes 24584 | tf_op jit(solution)/shard_map/ppermute | solution.py:88
  25.9 10.4 %collective-permute-start.4 = (f32[16,128]{1,0:T(8,128)S(1)}, f32[16,128]{1,0:T(8,128)S(1)}, u32[]{:S(2)}, u32[]{:S(2)}) collective-permute-start(f32[16,128]{1,0:T(8,128)S(1)} %broadcast_select_fusion.16), channel_id=1, source_target_pairs={{0,1},{1,0},{2,3},{3,2},{4,5},{5,4},{6,7},{7,6},{8,9},{9,8},{10,11... | collective-permute-start | bytes 24584 | tf_op jit(solution)/shard_map/ppermute | solution.py:87
  36.5 0.6 collective-permute-done.4
  38.4 1.3 collective-permute-start.6
  39.8 4.5 %collective-permute-start.7 = (f32[16,128]{1,0:T(8,128)S(1)}, f32[16,128]{1,0:T(8,128)S(1)}, u32[]{:S(2)}, u32[]{:S(2)}) collective-permute-start(f32[16,128]{1,0:T(8,128)S(1)} %pad_maximum_fusion.17), channel_id=1, source_target_pairs={{0,128},{128,256},{256,384},{384,512},{512,640},{640,768},{768,896... | collective-permute-start | bytes 24584 | tf_op jit(solution)/shard_map/ppermute | solution.py:77
  44.8 0.4 collective-permute-done.7
  45.3 1.3 collective-permute-start.8
  46.7 4.5 %collective-permute-start.9 = (f32[16,128]{1,0:T(8,128)S(1)}, f32[16,128]{1,0:T(8,128)S(1)}, u32[]{:S(2)}, u32[]{:S(2)}) collective-permute-start(f32[16,128]{1,0:T(8,128)S(1)} %pad_maximum_fusion.19), channel_id=1, source_target_pairs={{0,16},{16,32},{32,48},{48,64},{64,80},{80,96},{96,112},{1,17},{17... | collective-permute-start | bytes 24584 | tf_op jit(solution)/shard_map/ppermute | solution.py:77
  52.6 1.9 collective-permute-start.11
  54.5 2.7 %collective-permute-start.10 = (f32[16,128]{1,0:T(8,128)S(1)}, f32[16,128]{1,0:T(8,128)S(1)}, u32[]{:S(2)}, u32[]{:S(2)}) collective-permute-start(f32[16,128]{1,0:T(8,128)S(1)} %broadcast_select_fusion.12), channel_id=1, source_target_pairs={{0,1},{1,0},{2,3},{3,2},{4,5},{5,4},{6,7},{7,6},{8,9},{9,8},{10,11... | collective-permute-start | bytes 24584 | tf_op jit(solution)/shard_map/ppermute | solution.py:87
  57.5 0.5 collective-permute-done.10
  58.7 0.4 multiply_reduce_fusion.3
  59.9 0.7 broadcast_select_fusion.8
  60.6 5.9 %all-to-all-start = ((f32[8,16,128]{2,1,0:T(8,128)}), f32[8,16,128]{2,1,0:T(8,128)S(1)}, u32[]{:S(2)}, u32[]{:S(2)}) async-start(f32[8,16,128]{2,1,0:T(8,128)} %broadcast_select_fusion.8), calls=%async_computation | async-start | bytes 131072 | tf_op jit(solution)/shard_map/all_to_all | solution.py:97
  66.5 7.1 %all-to-all-done = f32[8,16,128]{2,1,0:T(8,128)S(1)} async-done(((f32[8,16,128]{2,1,0:T(8,128)}), f32[8,16,128]{2,1,0:T(8,128)S(1)}, u32[]{:S(2)}, u32[]{:S(2)}) %all-to-all-start) | async-done | bytes 65568 | tf_op jit(solution)/shard_map/all_to_all | solution.py:97
  74.2 0.7 broadcast_select_fusion.7
  74.9 10.3 %all-to-all-start.1 = ((f32[8,16,128]{2,1,0:T(8,128)}), f32[8,16,128]{2,1,0:T(8,128)S(1)}, u32[]{:S(2)}, u32[]{:S(2)}) async-start(f32[8,16,128]{2,1,0:T(8,128)} %broadcast_select_fusion.7), calls=%async_computation.1 | async-start | bytes 131072 | tf_op jit(solution)/shard_map/all_to_all | solution.py:97
  85.5 7.0 %all-to-all-done.1 = f32[8,16,128]{2,1,0:T(8,128)S(1)} async-done(((f32[8,16,128]{2,1,0:T(8,128)}), f32[8,16,128]{2,1,0:T(8,128)S(1)}, u32[]{:S(2)}, u32[]{:S(2)}) %all-to-all-start.1) | async-done | bytes 65568 | tf_op jit(solution)/shard_map/all_to_all | solution.py:97
  93.4 0.7 broadcast_select_fusion.2
  94.1 16.1 %all-to-all-start.2 = ((f32[16,16,128]{2,1,0:T(8,128)}), f32[16,16,128]{2,1,0:T(8,128)S(1)}, u32[]{:S(2)}, u32[]{:S(2)}) async-start(f32[16,16,128]{2,1,0:T(8,128)} %broadcast_select_fusion.2), calls=%async_computation.2 | async-start | bytes 262144 | tf_op jit(solution)/shard_map/all_to_all | solution.py:97
  110.3 8.7 %all-to-all-done.2 = f32[16,16,128]{2,1,0:T(8,128)S(1)} async-done(((f32[16,16,128]{2,1,0:T(8,128)}), f32[16,16,128]{2,1,0:T(8,128)S(1)}, u32[]{:S(2)}, u32[]{:S(2)}) %all-to-all-start.2) | async-done | bytes 131104 | tf_op jit(solution)/shard_map/all_to_all | solution.py:97
  120.0 0.4 multiply_reduce_fusion.2
  121.2 9.9 %all_to_all.45 = f32[8,16,128]{2,1,0:T(8,128)S(1)} all-to-all(f32[8,16,128]{2,1,0:T(8,128)S(1)} %broadcast_select_fusion.6), channel_id=1, replica_groups=mesh['gx'=8,'gy'=8,'gz'=16] {'gx'}, dimensions={0} | all-to-all | bytes 131072 | tf_op jit(solution)/shard_map/all_to_all | solution.py:97
  131.7 0.7 broadcast_select_fusion.5
  132.4 3.3 %all-to-all-start.4 = ((f32[8,16,128]{2,1,0:T(8,128)}), f32[8,16,128]{2,1,0:T(8,128)S(1)}, u32[]{:S(2)}, u32[]{:S(2)}) async-start(f32[8,16,128]{2,1,0:T(8,128)} %broadcast_select_fusion.5), calls=%async_computation.4 | async-start | bytes 131072 | tf_op jit(solution)/shard_map/all_to_all | solution.py:97
  136.1 6.9 %all-to-all-done.4 = f32[8,16,128]{2,1,0:T(8,128)S(1)} async-done(((f32[8,16,128]{2,1,0:T(8,128)}), f32[8,16,128]{2,1,0:T(8,128)S(1)}, u32[]{:S(2)}, u32[]{:S(2)}) %all-to-all-start.4) | async-done | bytes 65568 | tf_op jit(solution)/shard_map/all_to_all | solution.py:97
  143.9 0.7 broadcast_select_fusion.1
  144.6 5.4 %all-to-all-start.5 = ((f32[16,16,128]{2,1,0:T(8,128)}), f32[16,16,128]{2,1,0:T(8,128)S(1)}, u32[]{:S(2)}, u32[]{:S(2)}) async-start(f32[16,16,128]{2,1,0:T(8,128)} %broadcast_select_fusion.1), calls=%async_computation.5 | async-start | bytes 262144 | tf_op jit(solution)/shard_map/all_to_all | solution.py:97
  150.1 9.0 %all-to-all-done.5 = f32[16,16,128]{2,1,0:T(8,128)S(1)} async-done(((f32[16,16,128]{2,1,0:T(8,128)}), f32[16,16,128]{2,1,0:T(8,128)S(1)}, u32[]{:S(2)}, u32[]{:S(2)}) %all-to-all-start.5) | async-done | bytes 131104 | tf_op jit(solution)/shard_map/all_to_all | solution.py:97
  160.1 0.4 multiply_reduce_fusion.1
  161.3 10.5 %all_to_all.46 = f32[8,16,128]{2,1,0:T(8,128)S(1)} all-to-all(f32[8,16,128]{2,1,0:T(8,128)S(1)} %broadcast_select_fusion.4), channel_id=1, replica_groups=mesh['gx'=8,'gy'=8,'gz'=16] {'gx'}, dimensions={0} | all-to-all | bytes 131072 | tf_op jit(solution)/shard_map/all_to_all | solution.py:97
  172.4 0.7 broadcast_select_fusion.3
  173.1 3.3 %all-to-all-start.7 = ((f32[8,16,128]{2,1,0:T(8,128)}), f32[8,16,128]{2,1,0:T(8,128)S(1)}, u32[]{:S(2)}, u32[]{:S(2)}) async-start(f32[8,16,128]{2,1,0:T(8,128)} %broadcast_select_fusion.3), calls=%async_computation.7 | async-start | bytes 131072 | tf_op jit(solution)/shard_map/all_to_all | solution.py:97
  176.8 6.8 %all-to-all-done.7 = f32[8,16,128]{2,1,0:T(8,128)S(1)} async-done(((f32[8,16,128]{2,1,0:T(8,128)}), f32[8,16,128]{2,1,0:T(8,128)S(1)}, u32[]{:S(2)}, u32[]{:S(2)}) %all-to-all-start.7) | async-done | bytes 65568 | tf_op jit(solution)/shard_map/all_to_all | solution.py:97
  184.4 0.7 broadcast_select_fusion
  185.2 4.9 %all-to-all-start.8 = ((f32[16,16,128]{2,1,0:T(8,128)}), f32[16,16,128]{2,1,0:T(8,128)S(1)}, u32[]{:S(2)}, u32[]{:S(2)}) async-start(f32[16,16,128]{2,1,0:T(8,128)} %broadcast_select_fusion), calls=%async_computation.8 | async-start | bytes 262144 | tf_op jit(solution)/shard_map/all_to_all | solution.py:97
  190.3 9.0 %all-to-all-done.8 = f32[16,16,128]{2,1,0:T(8,128)S(1)} async-done(((f32[16,16,128]{2,1,0:T(8,128)}), f32[16,16,128]{2,1,0:T(8,128)S(1)}, u32[]{:S(2)}, u32[]{:S(2)}) %all-to-all-start.8) | async-done | bytes 131104 | tf_op jit(solution)/shard_map/all_to_all | solution.py:97
  200.3 0.7 copy.51
  200.9 0.7 copy.52
  (314 shorter events, 17.5 us)
Async XLA Ops:
  0.6 58.1 %copy-start = (bf16[1,1,1,768,768]{4,3,2,1,0:T(8,128)(2,1)S(1)}, bf16[1,1,1,768,768]{4,3,2,1,0:T(8,128)(2,1)}, u32[]{:S(2)}) copy-start(bf16[1,1,1,768,768]{4,3,2,1,0:T(8,128)(2,1)} %param.8) | copy-start | bytes 3538948
  0.6 37.1 %copy-start.2 = (f32[1,1,1,12,768]{4,2,3,1,0:T(1,128)S(1)}, f32[1,1,1,12,768]{4,2,3,1,0:T(1,128)}, u32[]{:S(2)}) copy-start(f32[1,1,1,12,768]{4,2,3,1,0:T(1,128)} %param.7) | copy-start | bytes 110596
  0.7 37.1 %copy-start.1 = (bf16[1,1,1,768,768]{4,3,2,1,0:T(8,128)(2,1)S(1)}, bf16[1,1,1,768,768]{4,3,2,1,0:T(8,128)(2,1)}, u32[]{:S(2)}) copy-start(bf16[1,1,1,768,768]{4,3,2,1,0:T(8,128)(2,1)} %param.9) | copy-start | bytes 3538948
  4.3 6.2 %collective-permute-start = (f32[16,128]{1,0:T(8,128)S(1)}, f32[16,128]{1,0:T(8,128)S(1)}, u32[]{:S(2)}, u32[]{:S(2)}) collective-permute-start(f32[16,128]{1,0:T(8,128)S(1)} %pad_maximum_fusion.4), channel_id=1, source_target_pairs={{128,0},{256,128},{384,256},{512,384},{640,512},{768,640},{896,768... | collective-permute-start | bytes 24584 | tf_op jit(solution)/shard_map/ppermute | solution.py:78
  5.8 5.3 %collective-permute-start.1 = (f32[16,128]{1,0:T(8,128)S(1)}, f32[16,128]{1,0:T(8,128)S(1)}, u32[]{:S(2)}, u32[]{:S(2)}) collective-permute-start(f32[16,128]{1,0:T(8,128)S(1)} %pad_maximum_fusion.5), channel_id=1, source_target_pairs={{0,128},{128,256},{256,384},{384,512},{512,640},{640,768},{768,896... | collective-permute-start | bytes 24584 | tf_op jit(solution)/shard_map/ppermute | solution.py:77
  11.3 5.8 %collective-permute-start.2 = (f32[16,128]{1,0:T(8,128)S(1)}, f32[16,128]{1,0:T(8,128)S(1)}, u32[]{:S(2)}, u32[]{:S(2)}) collective-permute-start(f32[16,128]{1,0:T(8,128)S(1)} %pad_maximum_fusion.6), channel_id=1, source_target_pairs={{16,0},{32,16},{48,32},{64,48},{80,64},{96,80},{112,96},{17,1},{33... | collective-permute-start | bytes 24584 | tf_op jit(solution)/shard_map/ppermute | solution.py:78
  12.6 5.0 %collective-permute-start.3 = (f32[16,128]{1,0:T(8,128)S(1)}, f32[16,128]{1,0:T(8,128)S(1)}, u32[]{:S(2)}, u32[]{:S(2)}) collective-permute-start(f32[16,128]{1,0:T(8,128)S(1)} %pad_maximum_fusion.7), channel_id=1, source_target_pairs={{0,16},{16,32},{32,48},{48,64},{64,80},{80,96},{96,112},{1,17},{17... | collective-permute-start | bytes 24584 | tf_op jit(solution)/shard_map/ppermute | solution.py:77
  18.1 18.4 %collective-permute-start.5 = (f32[16,128]{1,0:T(8,128)S(1)}, f32[16,128]{1,0:T(8,128)S(1)}, u32[]{:S(2)}, u32[]{:S(2)}) collective-permute-start(f32[16,128]{1,0:T(8,128)S(1)} %get-tuple-element.15), channel_id=1, source_target_pairs={{1,2},{2,1},{3,4},{4,3},{5,6},{6,5},{7,8},{8,7},{9,10},{10,9},{11,... | collective-permute-start | bytes 24584 | tf_op jit(solution)/shard_map/ppermute | solution.py:88
  25.9 11.2 %collective-permute-start.4 = (f32[16,128]{1,0:T(8,128)S(1)}, f32[16,128]{1,0:T(8,128)S(1)}, u32[]{:S(2)}, u32[]{:S(2)}) collective-permute-start(f32[16,128]{1,0:T(8,128)S(1)} %broadcast_select_fusion.16), channel_id=1, source_target_pairs={{0,1},{1,0},{2,3},{3,2},{4,5},{5,4},{6,7},{7,6},{8,9},{9,8},{10,11... | collective-permute-start | bytes 24584 | tf_op jit(solution)/shard_map/ppermute | solution.py:87
  38.4 6.3 %collective-permute-start.6 = (f32[16,128]{1,0:T(8,128)S(1)}, f32[16,128]{1,0:T(8,128)S(1)}, u32[]{:S(2)}, u32[]{:S(2)}) collective-permute-start(f32[16,128]{1,0:T(8,128)S(1)} %pad_maximum_fusion.16), channel_id=1, source_target_pairs={{128,0},{256,128},{384,256},{512,384},{640,512},{768,640},{896,768... | collective-permute-start | bytes 24584 | tf_op jit(solution)/shard_map/ppermute | solution.py:78
  39.8 5.3 %collective-permute-start.7 = (f32[16,128]{1,0:T(8,128)S(1)}, f32[16,128]{1,0:T(8,128)S(1)}, u32[]{:S(2)}, u32[]{:S(2)}) collective-permute-start(f32[16,128]{1,0:T(8,128)S(1)} %pad_maximum_fusion.17), channel_id=1, source_target_pairs={{0,128},{128,256},{256,384},{384,512},{512,640},{640,768},{768,896... | collective-permute-start | bytes 24584 | tf_op jit(solution)/shard_map/ppermute | solution.py:77
  45.3 6.2 %collective-permute-start.8 = (f32[16,128]{1,0:T(8,128)S(1)}, f32[16,128]{1,0:T(8,128)S(1)}, u32[]{:S(2)}, u32[]{:S(2)}) collective-permute-start(f32[16,128]{1,0:T(8,128)S(1)} %pad_maximum_fusion.18), channel_id=1, source_target_pairs={{16,0},{32,16},{48,32},{64,48},{80,64},{96,80},{112,96},{17,1},{33... | collective-permute-start | bytes 24584 | tf_op jit(solution)/shard_map/ppermute | solution.py:78
  46.7 5.3 %collective-permute-start.9 = (f32[16,128]{1,0:T(8,128)S(1)}, f32[16,128]{1,0:T(8,128)S(1)}, u32[]{:S(2)}, u32[]{:S(2)}) collective-permute-start(f32[16,128]{1,0:T(8,128)S(1)} %pad_maximum_fusion.19), channel_id=1, source_target_pairs={{0,16},{16,32},{32,48},{48,64},{64,80},{80,96},{96,112},{1,17},{17... | collective-permute-start | bytes 24584 | tf_op jit(solution)/shard_map/ppermute | solution.py:77
  52.6 5.0 %collective-permute-start.11 = (f32[16,128]{1,0:T(8,128)S(1)}, f32[16,128]{1,0:T(8,128)S(1)}, u32[]{:S(2)}, u32[]{:S(2)}) collective-permute-start(f32[16,128]{1,0:T(8,128)S(1)} %get-tuple-element.10), channel_id=1, source_target_pairs={{1,2},{2,1},{3,4},{4,3},{5,6},{6,5},{7,8},{8,7},{9,10},{10,9},{11,... | collective-permute-start | bytes 24584 | tf_op jit(solution)/shard_map/ppermute | solution.py:88
  54.5 3.5 %collective-permute-start.10 = (f32[16,128]{1,0:T(8,128)S(1)}, f32[16,128]{1,0:T(8,128)S(1)}, u32[]{:S(2)}, u32[]{:S(2)}) collective-permute-start(f32[16,128]{1,0:T(8,128)S(1)} %broadcast_select_fusion.12), channel_id=1, source_target_pairs={{0,1},{1,0},{2,3},{3,2},{4,5},{5,4},{6,7},{7,6},{8,9},{9,8},{10,11... | collective-permute-start | bytes 24584 | tf_op jit(solution)/shard_map/ppermute | solution.py:87
  60.6 13.0 %all-to-all-start = ((f32[8,16,128]{2,1,0:T(8,128)}), f32[8,16,128]{2,1,0:T(8,128)S(1)}, u32[]{:S(2)}, u32[]{:S(2)}) async-start(f32[8,16,128]{2,1,0:T(8,128)} %broadcast_select_fusion.8), calls=%async_computation | async-start | bytes 131072 | tf_op jit(solution)/shard_map/all_to_all | solution.py:97
  74.9 17.6 %all-to-all-start.1 = ((f32[8,16,128]{2,1,0:T(8,128)}), f32[8,16,128]{2,1,0:T(8,128)S(1)}, u32[]{:S(2)}, u32[]{:S(2)}) async-start(f32[8,16,128]{2,1,0:T(8,128)} %broadcast_select_fusion.7), calls=%async_computation.1 | async-start | bytes 131072 | tf_op jit(solution)/shard_map/all_to_all | solution.py:97
  94.1 24.9 %all-to-all-start.2 = ((f32[16,16,128]{2,1,0:T(8,128)}), f32[16,16,128]{2,1,0:T(8,128)S(1)}, u32[]{:S(2)}, u32[]{:S(2)}) async-start(f32[16,16,128]{2,1,0:T(8,128)} %broadcast_select_fusion.2), calls=%async_computation.2 | async-start | bytes 262144 | tf_op jit(solution)/shard_map/all_to_all | solution.py:97
  132.4 10.6 %all-to-all-start.4 = ((f32[8,16,128]{2,1,0:T(8,128)}), f32[8,16,128]{2,1,0:T(8,128)S(1)}, u32[]{:S(2)}, u32[]{:S(2)}) async-start(f32[8,16,128]{2,1,0:T(8,128)} %broadcast_select_fusion.5), calls=%async_computation.4 | async-start | bytes 131072 | tf_op jit(solution)/shard_map/all_to_all | solution.py:97
  144.6 14.6 %all-to-all-start.5 = ((f32[16,16,128]{2,1,0:T(8,128)}), f32[16,16,128]{2,1,0:T(8,128)S(1)}, u32[]{:S(2)}, u32[]{:S(2)}) async-start(f32[16,16,128]{2,1,0:T(8,128)} %broadcast_select_fusion.1), calls=%async_computation.5 | async-start | bytes 262144 | tf_op jit(solution)/shard_map/all_to_all | solution.py:97
  173.1 10.5 %all-to-all-start.7 = ((f32[8,16,128]{2,1,0:T(8,128)}), f32[8,16,128]{2,1,0:T(8,128)S(1)}, u32[]{:S(2)}, u32[]{:S(2)}) async-start(f32[8,16,128]{2,1,0:T(8,128)} %broadcast_select_fusion.3), calls=%async_computation.7 | async-start | bytes 131072 | tf_op jit(solution)/shard_map/all_to_all | solution.py:97
  185.2 14.1 %all-to-all-start.8 = ((f32[16,16,128]{2,1,0:T(8,128)}), f32[16,16,128]{2,1,0:T(8,128)S(1)}, u32[]{:S(2)}, u32[]{:S(2)}) async-start(f32[16,16,128]{2,1,0:T(8,128)} %broadcast_select_fusion), calls=%async_computation.8 | async-start | bytes 262144 | tf_op jit(solution)/shard_map/all_to_all | solution.py:97

commit v2 on v1

--- a/solution.py
+++ b/solution.py
@@ -89,57 +89,84 @@
     return jnp.where(even, far, near), jnp.where(even, near, far)
 
 
-def line_swap(axis, ahead, behind):
+def line_swap(axis, ahead, behind, live):
     count = lax.axis_size(axis)
-    place = lax.axis_index(axis)
-    target = lax.broadcasted_iota(jnp.int32, (count, 1, 1), 0)
-    sent = jnp.where(target > place, ahead[None], behind[None])
+    later, index_before, index_after = live["place"][axis]
+    sent = jnp.where(later, ahead[None], behind[None])
+    sent, live = lax.optimization_barrier((sent, live))
     got = lax.all_to_all(sent, axis, 0, 0, tiled=True)
-    before = lax.dynamic_index_in_dim(got, jnp.maximum(place - 1, 0), 0, keepdims=False)
-    after = lax.dynamic_index_in_dim(got, jnp.minimum(place + 1, count - 1), 0, keepdims=False)
-    return before, after, jnp.sum(got[:, 12:16, :], axis=0)
-
-
-def exchange(y, sums=()):
+    got, live = lax.optimization_barrier((got, live))
+    later, index_before, index_after = live["place"][axis]
+    before = lax.dynamic_index_in_dim(got, index_before, 0, keepdims=False)
+    after = lax.dynamic_index_in_dim(got, index_after, 0, keepdims=False)
+    low = jnp.sum(got[:, 12:16, :], axis=0)
+    before, after = lax.optimization_barrier((before, after))
+    return before, after, low, live
+
+
+def places():
+    found = {}
+    for axis in ("gx", "gy", "gz"):
+        count = lax.axis_size(axis)
+        place = lax.axis_index(axis)
+        target = lax.broadcasted_iota(jnp.int32, (count, 16, 128), 0)
+        found[axis] = (target > place, jnp.maximum(place - 1, 0), jnp.minimum(place + 1, count - 1))
+    return found
+
+
+def exchange(y, sums, live):
     swaps = (shift_swap, shift_swap, pair_swap)
+    live = dict(live, y=y)
 
     def swap(stage, axis, ahead, behind):
-        nonlocal sums
+        nonlocal sums, live
         ahead = pack(*ahead, sums)
         behind = pack(*behind, sums)
         if not sums:
             before, after = swaps[stage](axis, ahead, behind)
         else:
-            before, after, low = line_swap(axis, ahead, behind)
+            before, after, low, live = line_swap(axis, ahead, behind, live)
             rest = unfold(low)
             sums = [rest[:, 2 * EDGE + i : 2 * EDGE + i + 1] for i in range(len(sums))]
-        return unpack(before), unpack(after)
-
-    mx, px = swap(
+        live = dict(live, **{axis: (before, after)})
+
+    def from_neighbours(axis):
+        return [unpack(tile) for tile in live[axis]]
+
+    y = live["y"]
+    swap(
         0,
         "gx",
         (block(y, 1, 0, 0), block(y, 1, 1, 0), block(y, 1, -1, 0), block(y, 1, 0, 1), block(y, 1, 0, -1)),
         (block(y, -1, 0, 0), block(y, -1, 1, 0), block(y, -1, -1, 0), block(y, -1, 0, 1), block(y, -1, 0, -1)),
     )
-    my, py = swap(
+    y = live["y"]
+    mx, px = from_neighbours("gx")
+    swap(
         1,
         "gy",
         (block(y, 0, 1, 0), mx[1], px[1], block(y, 0, 1, 1), block(y, 0, 1, -1)),
         (block(y, 0, -1, 0), mx[2], px[2], block(y, 0, -1, 1), block(y, 0, -1, -1)),
     )
-    mz, pz = swap(
+    y = live["y"]
+    mx, px = from_neighbours("gx")
+    my, py = from_neighbours("gy")
+    swap(
         2,
         "gz",
         (block(y, 0, 0, 1), mx[3], px[3], my[3], py[3]),
         (block(y, 0, 0, -1), mx[4], px[4], my[4], py[4]),
     )
+    mx, px = from_neighbours("gx")
+    my, py = from_neighbours("gy")
+    mz, pz = from_neighbours("gz")
     pieces = [
         px[0], mx[0], py[0], my[0], pz[0], mz[0],
         py[2], my[2], py[1], my[1],
         pz[2], mz[2], pz[1], mz[1],
         pz[4], mz[4], pz[3], mz[3],
     ]
-    return jnp.concatenate(pieces, axis=1), sums
+    return live["y"] + jnp.concatenate(pieces, axis=1), sums, live
 
 
 def per_device(loads, dual_ops, precond, counts, signs):
@@ -153,38 +180,44 @@
     alive = (jnp.asarray(position, jnp.int32) < limits).astype(jnp.float32)
     signed = signs[0, 0, 0].astype(jnp.float32) * alive
 
-    def local(matrix, vector):
-        scaled = (signed * vector).astype(jnp.bfloat16)
-        return signed * jnp.dot(scaled, matrix, preferred_element_type=jnp.float32)
-
     def dot(left, right):
         return jnp.sum(left * right, axis=1, keepdims=True)
 
+    live = {"place": places(), "alive": alive, "signed": signed}
+    live["dual"] = dual_ops[0, 0, 0]
+    live["pre"] = precond[0, 0, 0]
+
     def assemble(contribution, sums=()):
-        beside, sums = exchange(contribution, sums)
-        return alive * (contribution + beside), sums
-
-    dual_matrix = dual_ops[0, 0, 0]
-    pre_matrix = precond[0, 0, 0]
-    residual, _ = assemble(alive * loads[0, 0, 0])
-    part = local(pre_matrix, residual)
-    gamma_part = dot(residual, part)
-    direction, _ = assemble(part)
-    part = local(dual_matrix, direction)
-    image, (gamma, curvature) = assemble(part, (gamma_part, dot(direction, part)))
+        nonlocal live
+        whole, sums, live = exchange(contribution, sums, live)
+        return live["alive"] * whole, sums
+
+    def local(name, vector):
+        signed = live["signed"]
+        scaled = (signed * vector).astype(jnp.bfloat16)
+        return signed * jnp.dot(scaled, live[name], preferred_element_type=jnp.float32)
+
+    live["residual"], _ = assemble(loads[0, 0, 0])
+    part = local("pre", live["residual"])
+    gamma_part = dot(live["residual"], part)
+    live["direction"], _ = assemble(part)
+    part = local("dual", live["direction"])
+    image, (gamma, curvature) = assemble(part, (gamma_part, dot(live["direction"], part)))
     step = gamma / curvature
-    multipliers = step * direction
-    residual = residual - step * image
+    live["multipliers"] = step * live["direction"]
+    live["residual"] = live["residual"] - step * image
+    live["gamma"] = gamma
     for _ in range(1, ITERS):
-        gamma_old = gamma
-        part = local(pre_matrix, residual)
-        smoothed, (gamma,) = assemble(part, (dot(residual, part),))
-        direction = smoothed + (gamma / gamma_old) * direction
-        part = local(dual_matrix, direction)
-        image, (curvature,) = assemble(part, (dot(direction, part),))
-        step = gamma / curvature
-        multipliers = multipliers + step * direction
-        residual = residual - step * image
+        part = local("pre", live["residual"])
+        smoothed, (gamma,) = assemble(part, (dot(live["residual"], part),))
+        live["direction"] = smoothed + (gamma / live["gamma"]) * live["direction"]
+        live["gamma"] = gamma
+        part = local("dual", live["direction"])
+        image, (curvature,) = assemble(part, (dot(live["direction"], part),))
+        step = live["gamma"] / curvature
+        live["multipliers"] = live["multipliers"] + step * live["direction"]
+        live["residual"] = live["residual"] - step * image
+    multipliers, residual = live["multipliers"], live["residual"]
     return (multipliers[None, None, None], residual[None, None, None])
 
 

time: 203 us -> 196 us (0.966)
  blocking collectives: 20.5 us -> 119 us
  starting transfers between devices: 94.9 us -> 41.8 us
  waiting for transfers between devices: 57.5 us -> 10 us
  other arithmetic: 15.3 us -> 9.32 us
    all_to_all x2 -> x9, blocking collectives: 20.5 us -> 119 us  [line_swap(): got = lax.all_to_all(sent, axis, 0, 0, tiled=True)]
    all_to_all x7 -> x0, waiting for transfers between devices: 54.6 us -> none  [line_swap(): got = lax.all_to_all(sent, axis, 0, 0, tiled=True)]
    all_to_all x7 -> x0, starting transfers between devices: 49.2 us -> none  [line_swap(): got = lax.all_to_all(sent, axis, 0, 0, tiled=True)]
    ppermute x4, waiting for transfers between devices: 0.01 us -> 5.6 us  [shift_swap(): after = lax.ppermute(behind, axis, [(i + 1, i) for i in range(ends)])]
    select_n x9, other arithmetic: 5.15 us -> 0.2 us  [line_swap(): sent = jnp.where(later, ahead[None], behind[None])]
    ppermute x4, starting transfers between devices: 17.8 us -> 13.4 us  [shift_swap(): before = lax.ppermute(ahead, axis, [(i, i + 1) for i in range(ends)])]
    ppermute x2, waiting for transfers between devices: 0.18 us -> 4.05 us  [pair_swap(): far = lax.ppermute(jnp.where(even, behind, ahead), axis, outer)]
    ppermute x2, starting transfers between devices: 13.1 us -> 16.8 us  [pair_swap(): near = lax.ppermute(jnp.where(even, ahead, behind), axis, inner)]
  transfers between devices with their start and end apart: 19 -> 12, of which waited for: 14 -> 5; matrix products, arithmetic and copies ran while one was open for 2% -> 2% of each run, Pallas kernels for 0% -> 0%
where the time goes in v2:
time: 196 us; the launch traced here: 195 us
  blocking collectives  119 us (61%)
  starting transfers between devices  41.8 us (21%)
  local copies, waits for them, and re-layouts  12.4 us (6%)
  waiting for transfers between devices  10 us (5%)
  other arithmetic  9.32 us (5%)
    all_to_all x9, blocking collectives, line_swap(): got = lax.all_to_all(sent, axis, 0, 0, tiled=True)  119 us
    ppermute x2, starting transfers between devices, pair_swap(): near = lax.ppermute(jnp.where(even, ahead, behind), axis, inner)  16.8 us
    ppermute x4, starting transfers between devices, shift_swap(): before = lax.ppermute(ahead, axis, [(i, i + 1) for i in range(ends)])  13.4 us
    ppermute x2, starting transfers between devices, pair_swap(): far = lax.ppermute(jnp.where(even, behind, ahead), axis, outer)  6.43 us
    ppermute x4, waiting for transfers between devices, shift_swap(): after = lax.ppermute(behind, axis, [(i + 1, i) for i in range(ends)])  5.6 us
    ppermute x4, starting transfers between devices, shift_swap(): after = lax.ppermute(behind, axis, [(i + 1, i) for i in range(ends)])  5.14 us
    ppermute x2, waiting for transfers between devices, pair_swap(): far = lax.ppermute(jnp.where(even, behind, ahead), axis, outer)  4.05 us
  transfers between devices with their start and end apart: 12, of which 5 were waited for; matrix products, arithmetic and copies ran while one was open for 2% of the time, Pallas kernels for 0%

profile of v2, /device:TPU:1, one launch (start us, length us, event | category | flops | bytes accessed | tf_op | source)
XLA Modules:
  0.0 195.3 jit_solution(8241109685098677002)
XLA Ops:
  0.7 0.9 copy.68
  1.9 1.3 collective-permute-start
  3.4 4.6 %collective-permute-start.1 = (f32[16,128]{1,0:T(8,128)S(1)}, f32[16,128]{1,0:T(8,128)S(1)}, u32[]{:S(2)}, u32[]{:S(2)}) collective-permute-start(f32[16,128]{1,0:T(8,128)S(1)} %pad_maximum_fusion.5), channel_id=1, source_target_pairs={{0,128},{128,256},{256,384},{384,512},{512,640},{640,768},{768,896... | collective-permute-start | bytes 24584 | tf_op jit(solution)/shard_map/ppermute | solution.py:77
  8.0 0.7 convert_reduce_fusion
  8.7 1.0 multiply_reduce_fusion
  9.7 0.7 broadcast_select_fusion.17
  10.8 3.5 %collective-permute-start.3 = (f32[16,128]{1,0:T(8,128)S(1)}, f32[16,128]{1,0:T(8,128)S(1)}, u32[]{:S(2)}, u32[]{:S(2)}) collective-permute-start(f32[16,128]{1,0:T(8,128)S(1)} %pad_maximum_fusion.7), channel_id=1, source_target_pairs={{0,16},{16,32},{32,48},{48,64},{64,80},{80,96},{96,112},{1,17},{17... | collective-permute-start | bytes 24584 | tf_op jit(solution)/shard_map/ppermute | solution.py:77
  14.4 1.3 collective-permute-start.2
  16.1 2.7 %collective-permute-done.2 = f32[16,128]{1,0:T(8,128)S(1)} collective-permute-done((f32[16,128]{1,0:T(8,128)S(1)}, f32[16,128]{1,0:T(8,128)S(1)}, u32[]{:S(2)}, u32[]{:S(2)}) %collective-permute-start.2) | collective-permute-done | bytes 8224 | tf_op jit(solution)/shard_map/ppermute | solution.py:78
  19.4 14.9 %collective-permute-start.4 = (f32[16,128]{1,0:T(8,128)S(1)}, f32[16,128]{1,0:T(8,128)S(1)}, u32[]{:S(2)}, u32[]{:S(2)}) collective-permute-start(f32[16,128]{1,0:T(8,128)S(1)} %broadcast_select_fusion.16), channel_id=1, source_target_pairs={{0,1},{1,0},{2,3},{3,2},{4,5},{5,4},{6,7},{7,6},{8,9},{9,8},{10,11... | collective-permute-start | bytes 24584 | tf_op jit(solution)/shard_map/ppermute | solution.py:87
  34.3 1.9 collective-permute-start.5
  36.4 2.9 %collective-permute-done.5 = f32[16,128]{1,0:T(8,128)S(1)} collective-permute-done((f32[16,128]{1,0:T(8,128)S(1)}, f32[16,128]{1,0:T(8,128)S(1)}, u32[]{:S(2)}, u32[]{:S(2)}) %collective-permute-start.5) | collective-permute-done | bytes 8224 | tf_op jit(solution)/shard_map/ppermute | solution.py:88
  39.7 0.1 concatenate.603
  39.9 0.3 convolution_multiply_fusion.3
  40.5 1.3 collective-permute-start.6
  42.0 4.0 %collective-permute-start.7 = (f32[16,128]{1,0:T(8,128)S(1)}, f32[16,128]{1,0:T(8,128)S(1)}, u32[]{:S(2)}, u32[]{:S(2)}) collective-permute-start(f32[16,128]{1,0:T(8,128)S(1)} %pad_maximum_fusion.17), channel_id=1, source_target_pairs={{0,128},{128,256},{256,384},{384,512},{512,640},{640,768},{768,896... | collective-permute-start | bytes 24584 | tf_op jit(solution)/shard_map/ppermute | solution.py:77
  46.1 0.1 concatenate.636
  46.4 0.3 collective-permute-done.7
  47.1 1.4 collective-permute-start.9
  48.5 1.3 collective-permute-start.8
  50.0 2.9 %collective-permute-done.8 = f32[16,128]{1,0:T(8,128)S(1)} collective-permute-done((f32[16,128]{1,0:T(8,128)S(1)}, f32[16,128]{1,0:T(8,128)S(1)}, u32[]{:S(2)}, u32[]{:S(2)}) %collective-permute-start.8) | collective-permute-done | bytes 8224 | tf_op jit(solution)/shard_map/ppermute | solution.py:78
  53.5 1.9 collective-permute-start.10
  55.4 4.5 %collective-permute-start.11 = (f32[16,128]{1,0:T(8,128)S(1)}, f32[16,128]{1,0:T(8,128)S(1)}, u32[]{:S(2)}, u32[]{:S(2)}) collective-permute-start(f32[16,128]{1,0:T(8,128)S(1)} %get-tuple-element.684), channel_id=1, source_target_pairs={{1,2},{2,1},{3,4},{4,3},{5,6},{6,5},{7,8},{8,7},{9,10},{10,9},{11,... | collective-permute-start | bytes 24584 | tf_op jit(solution)/shard_map/ppermute | solution.py:88
  60.1 1.2 collective-permute-done.11
  61.7 0.1 concatenate.634
  61.9 0.1 multiply_reduce_fusion.4
  62.0 0.4 multiply_reduce_fusion.3
  62.5 0.1 copy.43
  63.5 11.8 %all_to_all.45 = f32[8,16,128]{2,1,0:T(8,128)S(1)} all-to-all(f32[8,16,128]{2,1,0:T(8,128)S(1)} %broadcast_select_fusion.8), channel_id=1, replica_groups=mesh['gx'=8,'gy'=8,'gz'=16] {'gx'}, dimensions={0} | all-to-all | bytes 131072 | tf_op jit(solution)/shard_map/all_to_all | solution.py:97
  76.0 13.4 %all_to_all.46 = f32[8,16,128]{2,1,0:T(8,128)S(1)} all-to-all(f32[8,16,128]{2,1,0:T(8,128)S(1)} %broadcast_select_fusion.7), channel_id=1, replica_groups=mesh['gx'=8,'gy'=8,'gz'=16] {'gy'}, dimensions={0} | all-to-all | bytes 131072 | tf_op jit(solution)/shard_map/all_to_all | solution.py:97
  90.7 27.1 %all_to_all.47 = f32[16,16,128]{2,1,0:T(8,128)S(1)} all-to-all(f32[16,16,128]{2,1,0:T(8,128)S(1)} %broadcast_select_fusion.2), channel_id=1, replica_groups=mesh['gx'=8,'gy'=8,'gz'=16] {'gz'}, dimensions={0} | all-to-all | bytes 262144 | tf_op jit(solution)/shard_map/all_to_all | solution.py:97
  118.2 0.2 fusion.70
  118.7 0.1 concatenate.669
  118.9 0.4 multiply_reduce_fusion.2
  119.4 0.1 copy.47
  119.9 9.9 %all_to_all.48 = f32[8,16,128]{2,1,0:T(8,128)S(1)} all-to-all(f32[8,16,128]{2,1,0:T(8,128)S(1)} %broadcast_select_fusion.6), channel_id=1, replica_groups=mesh['gx'=8,'gy'=8,'gz'=16] {'gx'}, dimensions={0} | all-to-all | bytes 131072 | tf_op jit(solution)/shard_map/all_to_all | solution.py:97
  130.7 9.7 %all_to_all.49 = f32[8,16,128]{2,1,0:T(8,128)S(1)} all-to-all(f32[8,16,128]{2,1,0:T(8,128)S(1)} %broadcast_select_fusion.5), channel_id=1, replica_groups=mesh['gx'=8,'gy'=8,'gz'=16] {'gy'}, dimensions={0} | all-to-all | bytes 131072 | tf_op jit(solution)/shard_map/all_to_all | solution.py:97
  141.6 13.7 %all_to_all.50 = f32[16,16,128]{2,1,0:T(8,128)S(1)} all-to-all(f32[16,16,128]{2,1,0:T(8,128)S(1)} %broadcast_select_fusion.1), channel_id=1, replica_groups=mesh['gx'=8,'gy'=8,'gz'=16] {'gz'}, dimensions={0} | all-to-all | bytes 262144 | tf_op jit(solution)/shard_map/all_to_all | solution.py:97
  156.0 0.2 pad_maximum_fusion.2
  156.2 0.1 concatenate.702
  156.4 0.4 multiply_reduce_fusion.1
  157.5 10.5 %all_to_all.51 = f32[8,16,128]{2,1,0:T(8,128)S(1)} all-to-all(f32[8,16,128]{2,1,0:T(8,128)S(1)} %broadcast_select_fusion.4), channel_id=1, replica_groups=mesh['gx'=8,'gy'=8,'gz'=16] {'gx'}, dimensions={0} | all-to-all | bytes 131072 | tf_op jit(solution)/shard_map/all_to_all | solution.py:97
  168.8 9.6 %all_to_all.52 = f32[8,16,128]{2,1,0:T(8,128)S(1)} all-to-all(f32[8,16,128]{2,1,0:T(8,128)S(1)} %broadcast_select_fusion.3), channel_id=1, replica_groups=mesh['gx'=8,'gy'=8,'gz'=16] {'gy'}, dimensions={0} | all-to-all | bytes 131072 | tf_op jit(solution)/shard_map/all_to_all | solution.py:97
  179.6 13.2 %all_to_all.53 = f32[16,16,128]{2,1,0:T(8,128)S(1)} all-to-all(f32[16,16,128]{2,1,0:T(8,128)S(1)} %broadcast_select_fusion), channel_id=1, replica_groups=mesh['gx'=8,'gy'=8,'gz'=16] {'gz'}, dimensions={0} | all-to-all | bytes 262144 | tf_op jit(solution)/shard_map/all_to_all | solution.py:97
  193.6 0.2 fusion.12
  193.8 0.1 concatenate.737
  194.0 0.7 copy.52
  194.6 0.7 copy.51
  (310 shorter events, 15.6 us)
Async XLA Ops:
  0.6 61.4 %copy-start = (bf16[1,1,1,768,768]{4,3,2,1,0:T(8,128)(2,1)S(1)}, bf16[1,1,1,768,768]{4,3,2,1,0:T(8,128)(2,1)}, u32[]{:S(2)}) copy-start(bf16[1,1,1,768,768]{4,3,2,1,0:T(8,128)(2,1)} %param.8) | copy-start | bytes 3538948
  0.6 39.2 %copy-start.2 = (f32[1,1,1,12,768]{4,2,3,1,0:T(1,128)S(1)}, f32[1,1,1,12,768]{4,2,3,1,0:T(1,128)}, u32[]{:S(2)}) copy-start(f32[1,1,1,12,768]{4,2,3,1,0:T(1,128)} %param.7) | copy-start | bytes 110596
  0.7 39.2 %copy-start.1 = (bf16[1,1,1,768,768]{4,3,2,1,0:T(8,128)(2,1)S(1)}, bf16[1,1,1,768,768]{4,3,2,1,0:T(8,128)(2,1)}, u32[]{:S(2)}) copy-start(bf16[1,1,1,768,768]{4,3,2,1,0:T(8,128)(2,1)} %param.9) | copy-start | bytes 3538948
  1.9 8.6 %collective-permute-start = (f32[16,128]{1,0:T(8,128)S(1)}, f32[16,128]{1,0:T(8,128)S(1)}, u32[]{:S(2)}, u32[]{:S(2)}) collective-permute-start(f32[16,128]{1,0:T(8,128)S(1)} %pad_maximum_fusion.4), channel_id=1, source_target_pairs={{128,0},{256,128},{384,256},{512,384},{640,512},{768,640},{896,768... | collective-permute-start | bytes 24584 | tf_op jit(solution)/shard_map/ppermute | solution.py:78
  3.4 7.2 %collective-permute-start.1 = (f32[16,128]{1,0:T(8,128)S(1)}, f32[16,128]{1,0:T(8,128)S(1)}, u32[]{:S(2)}, u32[]{:S(2)}) collective-permute-start(f32[16,128]{1,0:T(8,128)S(1)} %pad_maximum_fusion.5), channel_id=1, source_target_pairs={{0,128},{128,256},{256,384},{384,512},{512,640},{640,768},{768,896... | collective-permute-start | bytes 24584 | tf_op jit(solution)/shard_map/ppermute | solution.py:77
  10.8 5.2 %collective-permute-start.3 = (f32[16,128]{1,0:T(8,128)S(1)}, f32[16,128]{1,0:T(8,128)S(1)}, u32[]{:S(2)}, u32[]{:S(2)}) collective-permute-start(f32[16,128]{1,0:T(8,128)S(1)} %pad_maximum_fusion.7), channel_id=1, source_target_pairs={{0,16},{16,32},{32,48},{48,64},{64,80},{80,96},{96,112},{1,17},{17... | collective-permute-start | bytes 24584 | tf_op jit(solution)/shard_map/ppermute | solution.py:77
  14.4 4.4 %collective-permute-start.2 = (f32[16,128]{1,0:T(8,128)S(1)}, f32[16,128]{1,0:T(8,128)S(1)}, u32[]{:S(2)}, u32[]{:S(2)}) collective-permute-start(f32[16,128]{1,0:T(8,128)S(1)} %pad_maximum_fusion.6), channel_id=1, source_target_pairs={{16,0},{32,16},{48,32},{64,48},{80,64},{96,80},{112,96},{17,1},{33... | collective-permute-start | bytes 24584 | tf_op jit(solution)/shard_map/ppermute | solution.py:78
  19.4 17.0 %collective-permute-start.4 = (f32[16,128]{1,0:T(8,128)S(1)}, f32[16,128]{1,0:T(8,128)S(1)}, u32[]{:S(2)}, u32[]{:S(2)}) collective-permute-start(f32[16,128]{1,0:T(8,128)S(1)} %broadcast_select_fusion.16), channel_id=1, source_target_pairs={{0,1},{1,0},{2,3},{3,2},{4,5},{5,4},{6,7},{7,6},{8,9},{9,8},{10,11... | collective-permute-start | bytes 24584 | tf_op jit(solution)/shard_map/ppermute | solution.py:87
  34.3 5.0 %collective-permute-start.5 = (f32[16,128]{1,0:T(8,128)S(1)}, f32[16,128]{1,0:T(8,128)S(1)}, u32[]{:S(2)}, u32[]{:S(2)}) collective-permute-start(f32[16,128]{1,0:T(8,128)S(1)} %get-tuple-element.689), channel_id=1, source_target_pairs={{1,2},{2,1},{3,4},{4,3},{5,6},{6,5},{7,8},{8,7},{9,10},{10,9},{11,... | collective-permute-start | bytes 24584 | tf_op jit(solution)/shard_map/ppermute | solution.py:88
  40.5 5.7 %collective-permute-start.6 = (f32[16,128]{1,0:T(8,128)S(1)}, f32[16,128]{1,0:T(8,128)S(1)}, u32[]{:S(2)}, u32[]{:S(2)}) collective-permute-start(f32[16,128]{1,0:T(8,128)S(1)} %pad_maximum_fusion.16), channel_id=1, source_target_pairs={{128,0},{256,128},{384,256},{512,384},{640,512},{768,640},{896,768... | collective-permute-start | bytes 24584 | tf_op jit(solution)/shard_map/ppermute | solution.py:78
  42.0 4.8 %collective-permute-start.7 = (f32[16,128]{1,0:T(8,128)S(1)}, f32[16,128]{1,0:T(8,128)S(1)}, u32[]{:S(2)}, u32[]{:S(2)}) collective-permute-start(f32[16,128]{1,0:T(8,128)S(1)} %pad_maximum_fusion.17), channel_id=1, source_target_pairs={{0,128},{128,256},{256,384},{384,512},{512,640},{640,768},{768,896... | collective-permute-start | bytes 24584 | tf_op jit(solution)/shard_map/ppermute | solution.py:77
  47.1 2.7 %collective-permute-start.9 = (f32[16,128]{1,0:T(8,128)S(1)}, f32[16,128]{1,0:T(8,128)S(1)}, u32[]{:S(2)}, u32[]{:S(2)}) collective-permute-start(f32[16,128]{1,0:T(8,128)S(1)} %pad_maximum_fusion.19), channel_id=1, source_target_pairs={{0,16},{16,32},{32,48},{48,64},{64,80},{80,96},{96,112},{1,17},{17... | collective-permute-start | bytes 24584 | tf_op jit(solution)/shard_map/ppermute | solution.py:77
  48.5 4.4 %collective-permute-start.8 = (f32[16,128]{1,0:T(8,128)S(1)}, f32[16,128]{1,0:T(8,128)S(1)}, u32[]{:S(2)}, u32[]{:S(2)}) collective-permute-start(f32[16,128]{1,0:T(8,128)S(1)} %pad_maximum_fusion.18), channel_id=1, source_target_pairs={{16,0},{32,16},{48,32},{64,48},{80,64},{96,80},{112,96},{17,1},{33... | collective-permute-start | bytes 24584 | tf_op jit(solution)/shard_map/ppermute | solution.py:78
  53.5 6.6 %collective-permute-start.10 = (f32[16,128]{1,0:T(8,128)S(1)}, f32[16,128]{1,0:T(8,128)S(1)}, u32[]{:S(2)}, u32[]{:S(2)}) collective-permute-start(f32[16,128]{1,0:T(8,128)S(1)} %broadcast_select_fusion.12), channel_id=1, source_target_pairs={{0,1},{1,0},{2,3},{3,2},{4,5},{5,4},{6,7},{7,6},{8,9},{9,8},{10,11... | collective-permute-start | bytes 24584 | tf_op jit(solution)/shard_map/ppermute | solution.py:87
  55.4 5.8 %collective-permute-start.11 = (f32[16,128]{1,0:T(8,128)S(1)}, f32[16,128]{1,0:T(8,128)S(1)}, u32[]{:S(2)}, u32[]{:S(2)}) collective-permute-start(f32[16,128]{1,0:T(8,128)S(1)} %get-tuple-element.684), channel_id=1, source_target_pairs={{1,2},{2,1},{3,4},{4,3},{5,6},{6,5},{7,8},{8,7},{9,10},{10,9},{11,... | collective-permute-start | bytes 24584 | tf_op jit(solution)/shard_map/ppermute | solution.py:88

commit v3 on v1

v3 whole, which is shorter than its diff:
```python
import jax
import jax.numpy as jnp
import numpy as np
from jax import lax
from jax.experimental import pallas as pl
from jax.experimental.pallas import tpu as pltpu
from jax.sharding import PartitionSpec as P

FACE = 96
EDGE = 16
ITERS = 2


DIRECTIONS = (
    (1, 0, 0),
    (-1, 0, 0),
    (0, 1, 0),
    (0, -1, 0),
    (0, 0, 1),
    (0, 0, -1),
    (1, 1, 0),
    (1, -1, 0),
    (-1, 1, 0),
    (-1, -1, 0),
    (1, 0, 1),
    (1, 0, -1),
    (-1, 0, 1),
    (-1, 0, -1),
    (0, 1, 1),
    (0, 1, -1),
    (0, -1, 1),
    (0, -1, -1),
)


def block_table():
    capacity = [FACE] * 6 + [EDGE] * 12
    offsets = [sum(capacity[:course]) for course in range(18)]
    return (capacity, offsets)


CAPACITY, OFFSETS = block_table()


def block(values, *heading):
    course = DIRECTIONS.index(heading)
    return values[:, OFFSETS[course] : OFFSETS[course] + CAPACITY[course]]


THIRD = 42


def pack(face, edge_a, edge_b, edge_c, edge_d, sums):
    top = jnp.concatenate([face, edge_a, edge_b], axis=1)
    rest = jnp.concatenate([edge_c, edge_d, *sums], axis=1)
    rest = jnp.pad(rest, ((0, 0), (0, THIRD - rest.shape[1])))
    low = jnp.concatenate([rest[0:4], rest[4:8], rest[8:12]], axis=1)
    low = jnp.pad(low, ((0, 0), (0, 128 - 3 * THIRD)))
    return jnp.concatenate([top, low], axis=0)


def unfold(low):
    return jnp.concatenate([low[:, THIRD * i : THIRD * (i + 1)] for i in range(3)], axis=0)


def unpack(tile):
    rest = unfold(tile[12:16])
    return (
        tile[:12, :FACE],
        tile[:12, FACE : FACE + EDGE],
        tile[:12, FACE + EDGE : FACE + 2 * EDGE],
        rest[:, :EDGE],
        rest[:, EDGE : 2 * EDGE],
    )


def messages(stage, y, mx, px, my, py, sums):
    if stage == 0:
        ahead = (block(y, 1, 0, 0), block(y, 1, 1, 0), block(y, 1, -1, 0), block(y, 1, 0, 1), block(y, 1, 0, -1))
        behind = (block(y, -1, 0, 0), block(y, -1, 1, 0), block(y, -1, -1, 0), block(y, -1, 0, 1), block(y, -1, 0, -1))
    elif stage == 1:
        ahead = (block(y, 0, 1, 0), mx[1], px[1], block(y, 0, 1, 1), block(y, 0, 1, -1))
        behind = (block(y, 0, -1, 0), mx[2], px[2], block(y, 0, -1, 1), block(y, 0, -1, -1))
    else:
        ahead = (block(y, 0, 0, 1), mx[3], px[3], my[3], py[3])
        behind = (block(y, 0, 0, -1), mx[4], px[4], my[4], py[4])
    return pack(*ahead, sums), pack(*behind, sums)


def beside(mx, px, my, py, mz, pz):
    pieces = [
        px[0], mx[0], py[0], my[0], pz[0], mz[0],
        py[2], my[2], py[1], my[1],
        pz[2], mz[2], pz[1], mz[1],
        pz[4], mz[4], pz[3], mz[3],
    ]
    return jnp.concatenate(pieces, axis=1)


AXES = ("gx", "gy", "gz")
TILE = jax.ShapeDtypeStruct((2, 16, 128), jnp.float32)


class Here:
    def __getitem__(self, stage):
        return lax.axis_index(AXES[stage])


HERE = Here()


def kernel_call(name, body, shapes, *operands, last=False):
    arrays = [pltpu.with_memory_space_constraint(value, pltpu.VMEM) for value in operands if value is not HERE]

    def kernel(*refs):
        given = iter(refs)
        results = body(*[HERE if value is HERE else next(given) for value in operands])
        for ref, result in zip(given, results):
            if isinstance(result, list):
                for i, part in enumerate(result):
                    ref[i] = part
            elif result.shape != ref.shape:
                lines = result.shape[1] // 128
                for i in range(lines):
                    ref[pl.ds(i, result.shape[0], stride=lines), :] = result[:, 128 * i : 128 * (i + 1)]
            else:
                ref[...] = result

    return pl.pallas_call(
        kernel,
        name=name,
        in_specs=[pl.BlockSpec(memory_space=pltpu.VMEM) for _ in arrays],
        out_specs=[pl.BlockSpec(memory_space=pltpu.VMEM) for _ in shapes],
        out_shape=[shape if last else pltpu.VMEM(shape.shape, shape.dtype) for shape in shapes],
    )(*arrays)


def spread(ahead, behind, place, count):
    return [jnp.where(place < i, ahead, behind) for i in range(count)]


def pair_of(tiles):
    return unpack(tiles[0]), unpack(tiles[1])


def permuted(axis, tiles, place):
    count = lax.axis_size(axis)
    if axis != "gz":
        before = lax.ppermute(tiles[0], axis, [(i, i + 1) for i in range(count - 1)])
        after = lax.ppermute(tiles[1], axis, [(i + 1, i) for i in range(count - 1)])
        return before, after
    near = lax.ppermute(tiles[0], axis, [(i, i ^ 1) for i in range(count)])
    far = lax.ppermute(tiles[1], axis, [(i, i + 1 if i % 2 else i - 1) for i in range(1, count - 1)])
    return near, far


def exchange_by_permutes(y, sent, place):
    tile = jax.ShapeDtypeStruct((16, 128), jnp.float32)
    x_tiles = permuted("gx", sent, place)

    def second(y, mx, px, place):
        return messages(1, y[...], unpack(mx[...]), unpack(px[...]), None, None, ())

    sent = kernel_call("second", second, (tile, tile), y, *x_tiles, place)
    y_tiles = permuted("gy", sent, place)

    def third(y, mx, px, my, py, place):
        ahead, behind = messages(2, y[...], *[unpack(v[...]) for v in (mx, px, my, py)], ())
        even = lax.rem(place[2], 2) == 0
        return jnp.where(even, ahead, behind), jnp.where(even, behind, ahead)

    sent = kernel_call("third", third, (tile, tile), y, *x_tiles, *y_tiles, place)
    return (*x_tiles, *y_tiles, *permuted("gz", sent, place))


def from_permutes(tiles, place):
    mx, px, my, py, near, far = [value[...] for value in tiles]
    even = lax.rem(place[2], 2) == 0
    mz, pz = jnp.where(even, far, near), jnp.where(even, near, far)
    return beside(*[unpack(value) for value in (mx, px, my, py, mz, pz)])


def gathered(stage, axis, sent, live):
    sent, live = lax.optimization_barrier((sent, live))
    got = lax.all_to_all(sent, axis, 0, 0, tiled=True)
    return lax.optimization_barrier((got, live))


def picked(got, place, stage, number):
    count = got.shape[0]
    here = place[stage]
    before = got[jnp.maximum(here - 1, 0)]
    after = got[jnp.minimum(here + 1, count - 1)]
    low = got[0, 12:16, :]
    for i in range(1, count):
        low = low + got[i, 12:16, :]
    rest = unfold(low)
    return before, after, [rest[:, 2 * EDGE + i : 2 * EDGE + i + 1] for i in range(number)]


def exchange_by_gathers(y, sent, place, number, live):
    sizes = [lax.axis_size(axis) for axis in AXES]

    def blocks(stage):
        return jax.ShapeDtypeStruct((sizes[stage], 16, 128), jnp.float32)

    live = dict(live, y=y)
    got, live = gathered(0, "gx", sent, live)

    def second(y, got, place):
        before, after, sums = picked(got, place, 0, number)
        ahead, behind = messages(1, y[...], unpack(before), unpack(after), None, None, sums)
        return spread(ahead, behind, place[1], sizes[1]), [before, after]

    sent, x_tiles = kernel_call("second_sum", second, (blocks(1), TILE), live["y"], got, HERE)
    live["x_tiles"] = x_tiles
    got, live = gathered(1, "gy", sent, live)

    def third(y, x_tiles, got, place):
        before, after, sums = picked(got, place, 1, number)
        ahead, behind = messages(2, y[...], *pair_of(x_tiles), unpack(before), unpack(after), sums)
        return spread(ahead, behind, place[2], sizes[2]), [before, after]

    sent, y_tiles = kernel_call("third_sum", third, (blocks(2), TILE), live["y"], live["x_tiles"], got, HERE)
    live["y_tiles"] = y_tiles
    return gathered(2, "gz", sent, live)


def from_gathers(got, x_tiles, y_tiles, place, number):
    before, after, sums = picked(got, place, 2, number)
    return beside(*pair_of(x_tiles), *pair_of(y_tiles), unpack(before), unpack(after)), sums


def per_device(loads, dual_ops, precond, counts, signs):
    order_max = sum(CAPACITY)
    owners = np.zeros((18, order_max), np.int32)
    position = np.zeros((order_max,), np.int32)
    for course in range(18):
        owners[course, OFFSETS[course] : OFFSETS[course] + CAPACITY[course]] = 1
        position[OFFSETS[course] : OFFSETS[course] + CAPACITY[course]] = np.arange(CAPACITY[course])
    limits = jnp.sum(counts[0, 0, 0][:, None] * jnp.asarray(owners, jnp.int32), axis=0)
    alive = (jnp.asarray(position, jnp.int32) < limits).astype(jnp.float32)[None]
    signed = signs[0, 0, 0].astype(jnp.float32)[None] * alive
    place = HERE
    dual, pre = dual_ops[0, 0, 0], precond[0, 0, 0]
    loads = loads[0, 0, 0]
    sizes = [lax.axis_size(axis) for axis in AXES]
    vector = jax.ShapeDtypeStruct(loads.shape, jnp.float32)
    rounded = jax.ShapeDtypeStruct(loads.shape, jnp.bfloat16)
    column = jax.ShapeDtypeStruct((loads.shape[0], 1), jnp.float32)
    tile = jax.ShapeDtypeStruct((16, 128), jnp.float32)
    first_blocks = jax.ShapeDtypeStruct((sizes[0], 16, 128), jnp.float32)

    def times(scaled, matrix):
        return jnp.dot(scaled, matrix, preferred_element_type=jnp.float32)

    def dot(left, right):
        return jnp.sum(left * right, axis=1, keepdims=True)

    def load_tiles(loads, place):
        return messages(0, loads[...], None, None, None, None, ())

    sent = kernel_call("load_tiles", load_tiles, (tile, tile), loads, place)
    tiles = exchange_by_permutes(loads, sent, place)

    def begin(y, alive, signed, place, *tiles):
        residual = alive[...] * (y[...] + from_permutes(tiles, place))
        return residual, (signed[...] * residual).astype(jnp.bfloat16)

    residual, scaled = kernel_call("begin", begin, (vector, rounded), loads, alive, signed, place, *tiles)

    def precond_tiles(product, signed, residual, place):
        y = signed[...] * product[...]
        return (y, dot(residual[...], y), *messages(0, y, None, None, None, None, ()))

    y, gamma_part, *sent = kernel_call(
        "precond_tiles", precond_tiles, (vector, column, tile, tile), times(scaled, pre), signed, residual, place
    )
    tiles = exchange_by_permutes(y, sent, place)

    def aim(y, alive, signed, place, *tiles):
        direction = alive[...] * (y[...] + from_permutes(tiles, place))
        return direction, (signed[...] * direction).astype(jnp.bfloat16)

    direction, scaled = kernel_call("aim", aim, (vector, rounded), y, alive, signed, place, *tiles)

    live = dict(alive=alive, signed=signed, residual=residual, direction=direction, dual=dual, pre=pre)

    def image_blocks(product, signed, direction, gamma_part, place):
        y = signed[...] * product[...]
        sums = (gamma_part[...], dot(direction[...], y))
        return y, spread(*messages(0, y, None, None, None, None, sums), place[0], sizes[0])

    y, sent = kernel_call(
        "image_blocks",
        image_blocks,
        (vector, first_blocks),
        times(scaled, live["dual"]),
        signed,
        direction,
        gamma_part,
        place,
    )
    got, live = exchange_by_gathers(y, sent, place, 2, live)

    def first_step(got, x_tiles, y_tiles, y, place, alive, signed, direction, residual):
        near, (gamma, curvature) = from_gathers(got, x_tiles, y_tiles, place, 2)
        image = alive[...] * (y[...] + near)
        step = gamma / curvature
        left = residual[...] - step * image
        return step * direction[...], left, (signed[...] * left).astype(jnp.bfloat16), gamma

    names = ("x_tiles", "y_tiles", "y", "place", "alive", "signed", "direction", "residual")
    live["multipliers"], live["residual"], scaled, live["gamma"] = kernel_call(
        "first_step", first_step, (vector, vector, rounded, column), got, *[live[name] if name != "place" else HERE for name in names]
    )

    def sum_blocks(product, signed, left, place):
        y = signed[...] * product[...]
        sums = (dot(left[...], y),)
        return y, spread(*messages(0, y, None, None, None, None, sums), place[0], sizes[0])

    for iteration in range(1, ITERS):
        y, sent = kernel_call(
            "smooth_blocks",
            sum_blocks,
            (vector, first_blocks),
            times(scaled, live["pre"]),
            live["signed"],
            live["residual"],
            HERE,
        )
        got, live = exchange_by_gathers(y, sent, HERE, 1, live)

        def turn(got, x_tiles, y_tiles, y, place, alive, signed, direction, gamma_old):
            near, (gamma,) = from_gathers(got, x_tiles, y_tiles, place, 1)
            smoothed = alive[...] * (y[...] + near)
            turned = smoothed + (gamma / gamma_old[...]) * direction[...]
            return turned, (signed[...] * turned).astype(jnp.bfloat16), gamma

        names = ("x_tiles", "y_tiles", "y", "place", "alive", "signed", "direction", "gamma")
        live["direction"], scaled, live["gamma"] = kernel_call(
            "turn", turn, (vector, rounded, column), got, *[live[name] if name != "place" else HERE for name in names]
        )
        y, sent = kernel_call(
            "sum_blocks",
            sum_blocks,
            (vector, first_blocks),
            times(scaled, live["dual"]),
            live["signed"],
            live["direction"],
            HERE,
        )
        got, live = exchange_by_gathers(y, sent, HERE, 1, live)

        def advance(got, x_tiles, y_tiles, y, place, alive, signed, direction, gamma, multipliers, residual):
            near, (curvature,) = from_gathers(got, x_tiles, y_tiles, place, 1)
            image = alive[...] * (y[...] + near)
            step = gamma[...] / curvature
            left = residual[...] - step * image
            results = (multipliers[...] + step * direction[...], left)
            if iteration < ITERS - 1:
                results += ((signed[...] * left).astype(jnp.bfloat16),)
            return results

        lines = jax.ShapeDtypeStruct((loads.size // 128, 128), jnp.float32)
        shapes = (vector, vector, rounded) if iteration < ITERS - 1 else (lines, lines)
        names = ("x_tiles", "y_tiles", "y", "place", "alive", "signed", "direction", "gamma", "multipliers", "residual")
        live["multipliers"], live["residual"], *rest = kernel_call(
            "advance",
            advance,
            shapes,
            got,
            *[live[name] if name != "place" else HERE for name in names],
            last=iteration == ITERS - 1,
        )
        if rest:
            scaled = rest[0]
    whole = (1, 1, 1, *loads.shape)
    return (live["multipliers"].reshape(whole), live["residual"].reshape(whole))


def solution(mesh):
    placed = (
        P("gx", "gy", "gz", None, None),
        P("gx", "gy", "gz", None, None),
        P("gx", "gy", "gz", None, None),
        P("gx", "gy", "gz", None),
        P("gx", "gy", "gz", None),
    )
    return jax.shard_map(
        per_device,
        mesh=mesh,
        in_specs=placed,
        out_specs=(P("gx", "gy", "gz", None, None), P("gx", "gy", "gz", None, None)),
        check_vma=False,
    )
```

time: 203 us -> 182 us (0.90)
  blocking collectives: 20.5 us -> 120 us
  starting transfers between devices: 94.9 us -> 37.4 us
  waiting for transfers between devices: 57.5 us -> 14.3 us
  other arithmetic: 15.3 us -> 2.37 us
  local copies, waits for them, and re-layouts: 10.7 us -> 0.95 us
  Pallas kernels: 0 us -> 4.32 us
    all_to_all x2 -> x9, blocking collectives: 20.5 us -> 120 us  [gathered(): got = lax.all_to_all(sent, axis, 0, 0, tiled=True)]
    all_to_all x7 -> x0, waiting for transfers between devices: 54.6 us -> none  [line_swap(): got = lax.all_to_all(sent, axis, 0, 0, tiled=True)]
    all_to_all x7 -> x0, starting transfers between devices: 49.2 us -> none  [line_swap(): got = lax.all_to_all(sent, axis, 0, 0, tiled=True)]
    ppermute x12, waiting for transfers between devices: 2.87 us -> 14.3 us  [the longest x4 10.7 us: permuted(): after = lax.ppermute(tiles[1], axis, [(i + 1, i) for i in range(count - 1)])]
    ppermute x12, starting transfers between devices: 45.7 us -> 37.4 us  [the longest x2 15.6 us: permuted(): near = lax.ppermute(tiles[0], axis, [(i, i ^ 1) for i in range(count)])]
    slice x150 -> x0, local copies, waits for them, and re-layouts: 8.14 us -> none  [the longest x39 2.86 us: unfold(): low[:, THIRD * i:THIRD * (i + 1)]]
    concatenate x100 -> x0, other arithmetic: 5.48 us -> none  [the longest x30 2.28 us: pack(): low = jnp.concatenate([rest[0:4], rest[4:8], rest[8:12]], axis=1)]
    select_n x15 -> x0, other arithmetic: 5.33 us -> none  [the longest x9 5.15 us: line_swap(): sent = jnp.where(target > place, ahead[None], behind[None])]
  transfers between devices with their start and end apart: 19 -> 12, of which waited for: 14 -> 6; matrix products, arithmetic and copies ran while one was open for 2% -> 1% of each run, Pallas kernels for 0% -> 0%
where the time goes in v3:
time: 182 us; the launch traced here: 181 us
  blocking collectives  120 us (66%)
  starting transfers between devices  37.4 us (21%)
  waiting for transfers between devices  14.3 us (8%)
  Pallas kernels  4.32 us (2%)
  other arithmetic  2.37 us (1%)
    all_to_all x9, blocking collectives, gathered(): got = lax.all_to_all(sent, axis, 0, 0, tiled=True)  120 us
    ppermute x2, starting transfers between devices, permuted(): near = lax.ppermute(tiles[0], axis, [(i, i ^ 1) for i in range(count)])  15.6 us
    ppermute x4, waiting for transfers between devices, permuted(): after = lax.ppermute(tiles[1], axis, [(i + 1, i) for i in range(count - 1)])  10.7 us
    ppermute x4, starting transfers between devices, permuted(): lax.ppermute(tiles[0], axis, [(i, i + 1) for i in range(count - 1)])  9.96 us
    ppermute x2, starting transfers between devices, permuted(): lax.ppermute(tiles[1], axis, [(i, i + 1 if i % 2 else i - 1) for i in ran...  6.72 us
    ppermute x4, starting transfers between devices, permuted(): after = lax.ppermute(tiles[1], axis, [(i + 1, i) for i in range(count - 1)])  5.17 us
    pallas_call x20, Pallas kernels, kernel_call(): pl.pallas_call(kernel, name=name, in_specs=[pl.BlockSpec(memory_space=plt...  4.32 us
  transfers between devices with their start and end apart: 12, of which 6 were waited for; matrix products, arithmetic and copies ran while one was open for 1% of the time, Pallas kernels for 0%

profile of v3, /device:TPU:1, one launch (start us, length us, event | category | flops | bytes accessed | tf_op | source)
XLA Modules:
  0.0 181.0 jit_solution(11229808920800552352)
XLA Ops:
  0.7 0.9 copy.17
  1.7 3.9 %collective-permute-start = (f32[16,128]{1,0:T(8,128)S(1)}, f32[16,128]{1,0:T(8,128)S(1)}, u32[]{:S(2)}, u32[]{:S(2)}) collective-permute-start(f32[16,128]{1,0:T(8,128)S(1)} %get-tuple-element.215), channel_id=1, source_target_pairs={{0,128},{128,256},{256,384},{384,512},{512,640},{640,768},{768,896... | collective-permute-start | bytes 24584 | tf_op jit(solution)/shard_map/ppermute | solution.py:149
  5.7 1.3 collective-permute-start.1
  7.0 1.0 multiply_reduce_fusion
  7.9 2.1 %collective-permute-done.1.refs_2_.refs_4_ = f32[16,128]{1,0:T(8,128)S(1)} collective-permute-done((f32[16,128]{1,0:T(8,128)S(1)}, f32[16,128]{1,0:T(8,128)S(1)}, u32[]{:S(2)}, u32[]{:S(2)}) %collective-permute-start.1) | collective-permute-done | bytes 8224 | tf_op jit(solution)/shard_map/ppermute | solution.py:150
  10.2 3.3 %collective-permute-start.2 = (f32[16,128]{1,0:T(8,128)S(1)}, f32[16,128]{1,0:T(8,128)S(1)}, u32[]{:S(2)}, u32[]{:S(2)}) collective-permute-start(f32[16,128]{1,0:T(8,128)S(1)} %get-tuple-element.217), channel_id=1, source_target_pairs={{0,16},{16,32},{32,48},{48,64},{64,80},{80,96},{96,112},{1,17},{17... | collective-permute-start | bytes 24584 | tf_op jit(solution)/shard_map/ppermute | solution.py:149
  13.5 1.3 collective-permute-start.3
  14.8 0.7 convert_reduce_fusion
  15.5 2.4 %collective-permute-done.3.refs_4_.refs_6_ = f32[16,128]{1,0:T(8,128)S(1)} collective-permute-done((f32[16,128]{1,0:T(8,128)S(1)}, f32[16,128]{1,0:T(8,128)S(1)}, u32[]{:S(2)}, u32[]{:S(2)}) %collective-permute-start.3) | collective-permute-done | bytes 8224 | tf_op jit(solution)/shard_map/ppermute | solution.py:150
  17.9 0.2 third.2
  18.1 13.7 %collective-permute-start.4 = (f32[16,128]{1,0:T(8,128)S(1)}, f32[16,128]{1,0:T(8,128)S(1)}, u32[]{:S(2)}, u32[]{:S(2)}) collective-permute-start(f32[16,128]{1,0:T(8,128)S(1)} %get-tuple-element.219), channel_id=1, source_target_pairs={{0,1},{1,0},{2,3},{3,2},{4,5},{5,4},{6,7},{7,6},{8,9},{9,8},{10,11... | collective-permute-start | bytes 24584 | tf_op jit(solution)/shard_map/ppermute | solution.py:152
  31.8 1.9 %collective-permute-start.5 = (f32[16,128]{1,0:T(8,128)S(1)}, f32[16,128]{1,0:T(8,128)S(1)}, u32[]{:S(2)}, u32[]{:S(2)}) collective-permute-start(f32[16,128]{1,0:T(8,128)S(1)} %get-tuple-element.220), channel_id=1, source_target_pairs={{1,2},{2,1},{3,4},{4,3},{5,6},{6,5},{7,8},{8,7},{9,10},{10,9},{11,... | collective-permute-start | bytes 24584 | tf_op jit(solution)/shard_map/ppermute | solution.py:153
  33.7 0.7 broadcast_select_fusion
  34.4 2.3 %collective-permute-done.5.refs_8_ = f32[16,128]{1,0:T(8,128)S(1)} collective-permute-done((f32[16,128]{1,0:T(8,128)S(1)}, f32[16,128]{1,0:T(8,128)S(1)}, u32[]{:S(2)}, u32[]{:S(2)}) %collective-permute-start.5) | collective-permute-done | bytes 8224 | tf_op jit(solution)/shard_map/ppermute | solution.py:153
  36.9 0.3 fusion.2.refs_0_
  37.2 0.2 precond_tiles.1
  37.4 1.4 collective-permute-start.6
  38.7 1.3 collective-permute-start.7
  40.0 3.1 %collective-permute-done.7.refs_2_.refs_4_ = f32[16,128]{1,0:T(8,128)S(1)} collective-permute-done((f32[16,128]{1,0:T(8,128)S(1)}, f32[16,128]{1,0:T(8,128)S(1)}, u32[]{:S(2)}, u32[]{:S(2)}) %collective-permute-start.7) | collective-permute-done | bytes 8224 | tf_op jit(solution)/shard_map/ppermute | solution.py:150
  43.3 1.4 collective-permute-start.8
  44.6 1.3 collective-permute-start.9
  45.9 3.1 %collective-permute-done.9.refs_4_.refs_6_ = f32[16,128]{1,0:T(8,128)S(1)} collective-permute-done((f32[16,128]{1,0:T(8,128)S(1)}, f32[16,128]{1,0:T(8,128)S(1)}, u32[]{:S(2)}, u32[]{:S(2)}) %collective-permute-start.9) | collective-permute-done | bytes 8224 | tf_op jit(solution)/shard_map/ppermute | solution.py:150
  49.0 0.2 third.3
  49.3 1.9 %collective-permute-start.10 = (f32[16,128]{1,0:T(8,128)S(1)}, f32[16,128]{1,0:T(8,128)S(1)}, u32[]{:S(2)}, u32[]{:S(2)}) collective-permute-start(f32[16,128]{1,0:T(8,128)S(1)} %get-tuple-element.228), channel_id=1, source_target_pairs={{0,1},{1,0},{2,3},{3,2},{4,5},{5,4},{6,7},{7,6},{8,9},{9,8},{10,11... | collective-permute-start | bytes 24584 | tf_op jit(solution)/shard_map/ppermute | solution.py:152
  51.2 4.8 %collective-permute-start.11 = (f32[16,128]{1,0:T(8,128)S(1)}, f32[16,128]{1,0:T(8,128)S(1)}, u32[]{:S(2)}, u32[]{:S(2)}) collective-permute-start(f32[16,128]{1,0:T(8,128)S(1)} %get-tuple-element.229), channel_id=1, source_target_pairs={{1,2},{2,1},{3,4},{4,3},{5,6},{6,5},{7,8},{8,7},{9,10},{10,9},{11,... | collective-permute-start | bytes 24584 | tf_op jit(solution)/shard_map/ppermute | solution.py:153
  56.0 1.3 collective-permute-done.11.refs_8_
  57.5 0.3 fusion.refs_0_
  57.8 0.2 image_blocks.1
  58.0 12.7 %all_to_all.45.refs_1_ = f32[8,16,128]{2,1,0:T(8,128)S(1)} all-to-all(f32[8,16,128]{2,1,0:T(8,128)S(1)} %get-tuple-element.235), channel_id=1, replica_groups=mesh['gx'=8,'gy'=8,'gz'=16] {'gx'}, dimensions={0} | all-to-all | bytes 131072 | tf_op jit(solution)/shard_map/all_to_all | solution.py:185
  70.7 0.2 second_sum.3
  70.9 13.4 %all_to_all.46.refs_2_ = f32[8,16,128]{2,1,0:T(8,128)S(1)} all-to-all(f32[8,16,128]{2,1,0:T(8,128)S(1)} %get-tuple-element.253), channel_id=1, replica_groups=mesh['gx'=8,'gy'=8,'gz'=16] {'gy'}, dimensions={0} | all-to-all | bytes 131072 | tf_op jit(solution)/shard_map/all_to_all | solution.py:185
  84.2 0.2 third_sum.3
  84.5 26.8 %all_to_all.47.refs_0_ = f32[16,16,128]{2,1,0:T(8,128)S(1)} all-to-all(f32[16,16,128]{2,1,0:T(8,128)S(1)} %get-tuple-element.273), channel_id=1, replica_groups=mesh['gx'=8,'gy'=8,'gz'=16] {'gz'}, dimensions={0} | all-to-all | bytes 262144 | tf_op jit(solution)/shard_map/all_to_all | solution.py:185
  111.3 0.2 first_step.1
  111.5 0.3 fusion.4.refs_0_
  111.8 0.2 smooth_blocks.1
  112.0 9.9 %all_to_all.48.refs_1_ = f32[8,16,128]{2,1,0:T(8,128)S(1)} all-to-all(f32[8,16,128]{2,1,0:T(8,128)S(1)} %get-tuple-element.299), channel_id=1, replica_groups=mesh['gx'=8,'gy'=8,'gz'=16] {'gx'}, dimensions={0} | all-to-all | bytes 131072 | tf_op jit(solution)/shard_map/all_to_all | solution.py:185
  122.1 9.7 %all_to_all.49.refs_2_ = f32[8,16,128]{2,1,0:T(8,128)S(1)} all-to-all(f32[8,16,128]{2,1,0:T(8,128)S(1)} %get-tuple-element.319), channel_id=1, replica_groups=mesh['gx'=8,'gy'=8,'gz'=16] {'gy'}, dimensions={0} | all-to-all | bytes 131072 | tf_op jit(solution)/shard_map/all_to_all | solution.py:185
  131.8 0.2 third_sum.4
  132.0 13.7 %all_to_all.50.refs_0_ = f32[16,16,128]{2,1,0:T(8,128)S(1)} all-to-all(f32[16,16,128]{2,1,0:T(8,128)S(1)} %get-tuple-element.341), channel_id=1, replica_groups=mesh['gx'=8,'gy'=8,'gz'=16] {'gz'}, dimensions={0} | all-to-all | bytes 262144 | tf_op jit(solution)/shard_map/all_to_all | solution.py:185
  145.7 0.2 turn.1
  145.9 0.3 fusion.5.refs_0_
  146.2 0.2 sum_blocks.1
  146.3 10.5 %all_to_all.51.refs_1_ = f32[8,16,128]{2,1,0:T(8,128)S(1)} all-to-all(f32[8,16,128]{2,1,0:T(8,128)S(1)} %get-tuple-element.368), channel_id=1, replica_groups=mesh['gx'=8,'gy'=8,'gz'=16] {'gx'}, dimensions={0} | all-to-all | bytes 131072 | tf_op jit(solution)/shard_map/all_to_all | solution.py:185
  157.0 9.6 %all_to_all.52.refs_2_ = f32[8,16,128]{2,1,0:T(8,128)S(1)} all-to-all(f32[8,16,128]{2,1,0:T(8,128)S(1)} %get-tuple-element.386), channel_id=1, replica_groups=mesh['gx'=8,'gy'=8,'gz'=16] {'gy'}, dimensions={0} | all-to-all | bytes 131072 | tf_op jit(solution)/shard_map/all_to_all | solution.py:185
  166.6 0.2 third_sum.5
  166.8 13.2 %all_to_all.53.refs_0_ = f32[16,16,128]{2,1,0:T(8,128)S(1)} all-to-all(f32[16,16,128]{2,1,0:T(8,128)S(1)} %get-tuple-element.406), channel_id=1, replica_groups=mesh['gx'=8,'gy'=8,'gz'=16] {'gz'}, dimensions={0} | all-to-all | bytes 262144 | tf_op jit(solution)/shard_map/all_to_all | solution.py:185
  180.1 0.9 advance.1
  (20 shorter events, 1.1 us)
Async XLA Ops:
  0.6 36.3 %copy-start = (bf16[1,1,1,768,768]{4,3,2,1,0:T(8,128)(2,1)S(1)}, bf16[1,1,1,768,768]{4,3,2,1,0:T(8,128)(2,1)}, u32[]{:S(2)}) copy-start(bf16[1,1,1,768,768]{4,3,2,1,0:T(8,128)(2,1)} %param.9) | copy-start | bytes 3538948
  0.6 56.8 %copy-start.1 = (bf16[1,1,1,768,768]{4,3,2,1,0:T(8,128)(2,1)S(1)}, bf16[1,1,1,768,768]{4,3,2,1,0:T(8,128)(2,1)}, u32[]{:S(2)}) copy-start(bf16[1,1,1,768,768]{4,3,2,1,0:T(8,128)(2,1)} %param.8) | copy-start | bytes 3538948
  1.7 6.2 %collective-permute-start = (f32[16,128]{1,0:T(8,128)S(1)}, f32[16,128]{1,0:T(8,128)S(1)}, u32[]{:S(2)}, u32[]{:S(2)}) collective-permute-start(f32[16,128]{1,0:T(8,128)S(1)} %get-tuple-element.215), channel_id=1, source_target_pairs={{0,128},{128,256},{256,384},{384,512},{512,640},{640,768},{768,896... | collective-permute-start | bytes 24584 | tf_op jit(solution)/shard_map/ppermute | solution.py:149
  5.7 4.4 %collective-permute-start.1 = (f32[16,128]{1,0:T(8,128)S(1)}, f32[16,128]{1,0:T(8,128)S(1)}, u32[]{:S(2)}, u32[]{:S(2)}) collective-permute-start(f32[16,128]{1,0:T(8,128)S(1)} %get-tuple-element.216), channel_id=1, source_target_pairs={{128,0},{256,128},{384,256},{512,384},{640,512},{768,640},{896,768... | collective-permute-start | bytes 24584 | tf_op jit(solution)/shard_map/ppermute | solution.py:150
  10.2 5.3 %collective-permute-start.2 = (f32[16,128]{1,0:T(8,128)S(1)}, f32[16,128]{1,0:T(8,128)S(1)}, u32[]{:S(2)}, u32[]{:S(2)}) collective-permute-start(f32[16,128]{1,0:T(8,128)S(1)} %get-tuple-element.217), channel_id=1, source_target_pairs={{0,16},{16,32},{32,48},{48,64},{64,80},{80,96},{96,112},{1,17},{17... | collective-permute-start | bytes 24584 | tf_op jit(solution)/shard_map/ppermute | solution.py:149
  13.5 4.4 %collective-permute-start.3 = (f32[16,128]{1,0:T(8,128)S(1)}, f32[16,128]{1,0:T(8,128)S(1)}, u32[]{:S(2)}, u32[]{:S(2)}) collective-permute-start(f32[16,128]{1,0:T(8,128)S(1)} %get-tuple-element.218), channel_id=1, source_target_pairs={{16,0},{32,16},{48,32},{64,48},{80,64},{96,80},{112,96},{17,1},{33... | collective-permute-start | bytes 24584 | tf_op jit(solution)/shard_map/ppermute | solution.py:150
  18.1 16.3 %collective-permute-start.4 = (f32[16,128]{1,0:T(8,128)S(1)}, f32[16,128]{1,0:T(8,128)S(1)}, u32[]{:S(2)}, u32[]{:S(2)}) collective-permute-start(f32[16,128]{1,0:T(8,128)S(1)} %get-tuple-element.219), channel_id=1, source_target_pairs={{0,1},{1,0},{2,3},{3,2},{4,5},{5,4},{6,7},{7,6},{8,9},{9,8},{10,11... | collective-permute-start | bytes 24584 | tf_op jit(solution)/shard_map/ppermute | solution.py:152
  31.8 5.0 %collective-permute-start.5 = (f32[16,128]{1,0:T(8,128)S(1)}, f32[16,128]{1,0:T(8,128)S(1)}, u32[]{:S(2)}, u32[]{:S(2)}) collective-permute-start(f32[16,128]{1,0:T(8,128)S(1)} %get-tuple-element.220), channel_id=1, source_target_pairs={{1,2},{2,1},{3,4},{4,3},{5,6},{6,5},{7,8},{8,7},{9,10},{10,9},{11,... | collective-permute-start | bytes 24584 | tf_op jit(solution)/shard_map/ppermute | solution.py:153
  37.4 2.7 %collective-permute-start.6 = (f32[16,128]{1,0:T(8,128)S(1)}, f32[16,128]{1,0:T(8,128)S(1)}, u32[]{:S(2)}, u32[]{:S(2)}) collective-permute-start(f32[16,128]{1,0:T(8,128)S(1)} %get-tuple-element.224), channel_id=1, source_target_pairs={{0,128},{128,256},{256,384},{384,512},{512,640},{640,768},{768,896... | collective-permute-start | bytes 24584 | tf_op jit(solution)/shard_map/ppermute | solution.py:149
  38.7 4.4 %collective-permute-start.7 = (f32[16,128]{1,0:T(8,128)S(1)}, f32[16,128]{1,0:T(8,128)S(1)}, u32[]{:S(2)}, u32[]{:S(2)}) collective-permute-start(f32[16,128]{1,0:T(8,128)S(1)} %get-tuple-element.225), channel_id=1, source_target_pairs={{128,0},{256,128},{384,256},{512,384},{640,512},{768,640},{896,768... | collective-permute-start | bytes 24584 | tf_op jit(solution)/shard_map/ppermute | solution.py:150
  43.3 2.7 %collective-permute-start.8 = (f32[16,128]{1,0:T(8,128)S(1)}, f32[16,128]{1,0:T(8,128)S(1)}, u32[]{:S(2)}, u32[]{:S(2)}) collective-permute-start(f32[16,128]{1,0:T(8,128)S(1)} %get-tuple-element.226), channel_id=1, source_target_pairs={{0,16},{16,32},{32,48},{48,64},{64,80},{80,96},{96,112},{1,17},{17... | collective-permute-start | bytes 24584 | tf_op jit(solution)/shard_map/ppermute | solution.py:149
  44.6 4.4 %collective-permute-start.9 = (f32[16,128]{1,0:T(8,128)S(1)}, f32[16,128]{1,0:T(8,128)S(1)}, u32[]{:S(2)}, u32[]{:S(2)}) collective-permute-start(f32[16,128]{1,0:T(8,128)S(1)} %get-tuple-element.227), channel_id=1, source_target_pairs={{16,0},{32,16},{48,32},{64,48},{80,64},{96,80},{112,96},{17,1},{33... | collective-permute-start | bytes 24584 | tf_op jit(solution)/shard_map/ppermute | solution.py:150
  49.3 6.7 %collective-permute-start.10 = (f32[16,128]{1,0:T(8,128)S(1)}, f32[16,128]{1,0:T(8,128)S(1)}, u32[]{:S(2)}, u32[]{:S(2)}) collective-permute-start(f32[16,128]{1,0:T(8,128)S(1)} %get-tuple-element.228), channel_id=1, source_target_pairs={{0,1},{1,0},{2,3},{3,2},{4,5},{5,4},{6,7},{7,6},{8,9},{9,8},{10,11... | collective-permute-start | bytes 24584 | tf_op jit(solution)/shard_map/ppermute | solution.py:152
  51.2 6.1 %collective-permute-start.11 = (f32[16,128]{1,0:T(8,128)S(1)}, f32[16,128]{1,0:T(8,128)S(1)}, u32[]{:S(2)}, u32[]{:S(2)}) collective-permute-start(f32[16,128]{1,0:T(8,128)S(1)} %get-tuple-element.229), channel_id=1, source_target_pairs={{1,2},{2,1},{3,4},{4,3},{5,6},{6,5},{7,8},{8,7},{9,10},{10,9},{11,... | collective-permute-start | bytes 24584 | tf_op jit(solution)/shard_map/ppermute | solution.py:153

commit v4 on v3

--- a/solution.py
+++ b/solution.py
@@ -118,7 +118,11 @@
         for ref, result in zip(given, results):
             if isinstance(result, list):
                 for i, part in enumerate(result):
-                    ref[i] = part
+                    at, part = part if isinstance(part, tuple) else (i, part)
+                    if part is None or part.shape != ref.shape[1:]:
+                        ref[at] = jnp.zeros(ref.shape[1:], ref.dtype)
+                    if part is not None:
+                        ref[at, : part.shape[0], : part.shape[1]] = part
             elif result.shape != ref.shape:
                 lines = result.shape[1] // 128
                 for i in range(lines):
@@ -143,41 +147,140 @@
     return unpack(tiles[0]), unpack(tiles[1])
 
 
-def permuted(axis, tiles, place):
-    count = lax.axis_size(axis)
-    if axis != "gz":
-        before = lax.ppermute(tiles[0], axis, [(i, i + 1) for i in range(count - 1)])
-        after = lax.ppermute(tiles[1], axis, [(i + 1, i) for i in range(count - 1)])
-        return before, after
-    near = lax.ppermute(tiles[0], axis, [(i, i ^ 1) for i in range(count)])
-    far = lax.ppermute(tiles[1], axis, [(i, i + 1 if i % 2 else i - 1) for i in range(1, count - 1)])
-    return near, far
-
-
-def exchange_by_permutes(y, sent, place):
-    tile = jax.ShapeDtypeStruct((16, 128), jnp.float32)
-    x_tiles = permuted("gx", sent, place)
-
-    def second(y, mx, px, place):
-        return messages(1, y[...], unpack(mx[...]), unpack(px[...]), None, None, ())
-
-    sent = kernel_call("second", second, (tile, tile), y, *x_tiles, place)
-    y_tiles = permuted("gy", sent, place)
-
-    def third(y, mx, px, my, py, place):
-        ahead, behind = messages(2, y[...], *[unpack(v[...]) for v in (mx, px, my, py)], ())
-        even = lax.rem(place[2], 2) == 0
-        return jnp.where(even, ahead, behind), jnp.where(even, behind, ahead)
-
-    sent = kernel_call("third", third, (tile, tile), y, *x_tiles, *y_tiles, place)
-    return (*x_tiles, *y_tiles, *permuted("gz", sent, place))
-
-
-def from_permutes(tiles, place):
-    mx, px, my, py, near, far = [value[...] for value in tiles]
-    even = lax.rem(place[2], 2) == 0
-    mz, pz = jnp.where(even, far, near), jnp.where(even, near, far)
-    return beside(*[unpack(value) for value in (mx, px, my, py, mz, pz)])
+MASK = (4, 2, 1)
+PAIRS = ((0, 1), (0, 2), (1, 2))
+
+
+def cubes(kind):
+    sizes = [lax.axis_size(axis) for axis in AXES]
+    found = {}
+    for place in np.ndindex(*sizes):
+        corner = tuple((i + kind) // 2 % (size // 2) for i, size in zip(place, sizes))
+        member = sum(mask * (i % 2) for mask, i in zip(MASK, place))
+        found.setdefault(corner, {})[member] = int(np.ravel_multi_index(place, sizes))
+    return [[members[i] for i in range(8)] for members in found.values()]
+
+
+def heading_of(signs_by_axis):
+    return tuple(signs_by_axis.get(axis, 0) for axis in range(3))
+
+
+class Parity:
+    def __init__(self, place):
+        parities = [lax.rem(place[axis], 2) for axis in range(3)]
+        self.even = [value == 0 for value in parities]
+        self.position = sum(mask * value for mask, value in zip(MASK, parities))
+
+    def choose(self, axes, values):
+        if len(axes) == 1:
+            return jnp.where(self.even[axes[0]], values(0), values(1))
+        return jnp.where(
+            self.even[axes[0]],
+            jnp.where(self.even[axes[1]], values(0, 0), values(0, 1)),
+            jnp.where(self.even[axes[1]], values(1, 0), values(1, 1)),
+        )
+
+    def own(self, y, axes, kinds):
+        def value(*odd):
+            return block(y, *heading_of({axis: 1 - 2 * (kind ^ i) for axis, kind, i in zip(axes, kinds, odd)}))
+
+        return self.choose(axes, value)
+
+    def toward(self, axes, signs, by_kinds):
+        return self.choose(axes, lambda *odd: by_kinds[tuple(sign ^ i for sign, i in zip(signs, odd))])
+
+
+def cube_b(y, parity):
+    sent = []
+    for axis in range(3):
+        rest = [other for other in range(3) if other != axis]
+        parts = [parity.own(y, (axis,), (1,))]
+        for other in rest:
+            first, second = sorted((axis, other))
+            parts.append(parity.own(y, (first, second), (int(first == axis), int(second == axis))))
+        sent.append((MASK[axis], jnp.concatenate(parts, axis=1)))
+    for pair in PAIRS:
+        sent.append((MASK[pair[0]] | MASK[pair[1]], parity.own(y, pair, (1, 1))))
+    return sent
+
+
+def members(got, parity):
+    return {mask: got[parity.position ^ mask][:12] for mask in range(1, 7)}
+
+
+def edge_at(tile, number):
+    return tile[:, FACE + EDGE * number : FACE + EDGE * (number + 1)]
+
+
+def passed(axis, other):
+    return [i for i in range(3) if i != axis].index(other)
+
+
+def cube_a(y, parity, from_b):
+    sent = []
+    for axis in range(3):
+        parts = [parity.own(y, (axis,), (0,))]
+        for other in range(3):
+            if other != axis:
+                parts.append(edge_at(from_b[MASK[other]], passed(other, axis)))
+        sent.append((MASK[axis], jnp.concatenate(parts, axis=1)))
+    for pair in PAIRS:
+        sent.append((MASK[pair[0]] | MASK[pair[1]], parity.own(y, pair, (0, 0))))
+    return sent
+
+
+def cube_beside(parity, from_a, from_b):
+    faces, edges = {}, {}
+    for axis in range(3):
+        by_kinds = {(0,): from_a[MASK[axis]][:, :FACE], (1,): from_b[MASK[axis]][:, :FACE]}
+        for sign in range(2):
+            faces[heading_of({axis: 1 - 2 * sign})] = parity.toward((axis,), (sign,), by_kinds)
+    for pair in PAIRS:
+        mask = MASK[pair[0]] | MASK[pair[1]]
+        first, second = pair
+        by_kinds = {
+            (0, 0): from_a[mask][:, :EDGE],
+            (1, 1): from_b[mask][:, :EDGE],
+            (0, 1): edge_at(from_a[MASK[first]], passed(first, second)),
+            (1, 0): edge_at(from_a[MASK[second]], passed(second, first)),
+        }
+        for signs in np.ndindex(2, 2):
+            heading = heading_of({axis: 1 - 2 * sign for axis, sign in zip(pair, signs)})
+            edges[heading] = parity.toward(pair, signs, by_kinds)
+    return jnp.concatenate([{**faces, **edges}[heading] for heading in DIRECTIONS], axis=1)
+
+
+def placed(sent, parity):
+    blocks = {mask: value for mask, value in sent}
+    return [(parity.position ^ mask, blocks.get(mask)) for mask in range(8)]
+
+
+def cube_swap(kind, sent, live):
+    sent, live = lax.optimization_barrier((sent, live))
+    got = lax.all_to_all(sent, AXES, 0, 0, axis_index_groups=cubes(kind), tiled=True)
+    return lax.optimization_barrier((got, live))
+
+
+CUBE = jax.ShapeDtypeStruct((8, 16, 128), jnp.float32)
+
+
+def exchange_by_cubes(sent, live):
+    got, live = cube_swap(1, sent, live)
+    live["from_b"] = got
+
+    def second(y, from_b):
+        parity = Parity(HERE)
+        return (placed(cube_a(y[...], parity, members(from_b, parity)), parity),)
+
+    (sent,) = kernel_call("cube_a", second, (CUBE,), live["y"], live["from_b"])
+    got, live = cube_swap(0, sent, live)
+    live["from_a"] = got
+    return live
+
+
+def from_cubes(from_a, from_b):
+    parity = Parity(HERE)
+    return cube_beside(parity, members(from_a, parity), members(from_b, parity))
 
 
 def gathered(stage, axis, sent, live):
@@ -232,15 +335,6 @@
 
 
 def per_device(loads, dual_ops, precond, counts, signs):
-    order_max = sum(CAPACITY)
-    owners = np.zeros((18, order_max), np.int32)
-    position = np.zeros((order_max,), np.int32)
-    for course in range(18):
-        owners[course, OFFSETS[course] : OFFSETS[course] + CAPACITY[course]] = 1
-        position[OFFSETS[course] : OFFSETS[course] + CAPACITY[course]] = np.arange(CAPACITY[course])
-    limits = jnp.sum(counts[0, 0, 0][:, None] * jnp.asarray(owners, jnp.int32), axis=0)
-    alive = (jnp.asarray(position, jnp.int32) < limits).astype(jnp.float32)[None]
-    signed = signs[0, 0, 0].astype(jnp.float32)[None] * alive
     place = HERE
     dual, pre = dual_ops[0, 0, 0], precond[0, 0, 0]
     loads = loads[0, 0, 0]
@@ -248,7 +342,6 @@
     vector = jax.ShapeDtypeStruct(loads.shape, jnp.float32)
     rounded = jax.ShapeDtypeStruct(loads.shape, jnp.bfloat16)
     column = jax.ShapeDtypeStruct((loads.shape[0], 1), jnp.float32)
-    tile = jax.ShapeDtypeStruct((16, 128), jnp.float32)
     first_blocks = jax.ShapeDtypeStruct((sizes[0], 16, 128), jnp.float32)
 
     def times(scaled, matrix):
@@ -257,34 +350,46 @@
     def dot(left, right):
         return jnp.sum(left * right, axis=1, keepdims=True)
 
-    def load_tiles(loads, place):
-        return messages(0, loads[...], None, None, None, None, ())
-
-    sent = kernel_call("load_tiles", load_tiles, (tile, tile), loads, place)
-    tiles = exchange_by_permutes(loads, sent, place)
-
-    def begin(y, alive, signed, place, *tiles):
-        residual = alive[...] * (y[...] + from_permutes(tiles, place))
-        return residual, (signed[...] * residual).astype(jnp.bfloat16)
-
-    residual, scaled = kernel_call("begin", begin, (vector, rounded), loads, alive, signed, place, *tiles)
-
-    def precond_tiles(product, signed, residual, place):
+    def load_blocks(loads, counts, signs):
+        position = lax.broadcasted_iota(jnp.int32, (1, FACE), 1)
+        alive = [
+            (position[:, : CAPACITY[course]] < counts[:, course : course + 1]).astype(jnp.float32)
+            for course in range(len(DIRECTIONS))
+        ]
+        alive = jnp.concatenate(alive, axis=1)
+        parity = Parity(HERE)
+        return alive, signs[...].astype(jnp.float32) * alive, placed(cube_b(loads[...], parity), parity)
+
+    row = jax.ShapeDtypeStruct((1, loads.shape[1]), jnp.float32)
+    live = dict(dual=dual, pre=pre)
+    live["alive"], live["signed"], sent = kernel_call(
+        "load_blocks", load_blocks, (row, row, CUBE), loads, counts[0, 0], signs[0, 0]
+    )
+    live["y"] = loads
+    live = exchange_by_cubes(sent, live)
+
+    def assemble(y, alive, signed, from_a, from_b):
+        whole = alive[...] * (y[...] + from_cubes(from_a, from_b))
+        return whole, (signed[...] * whole).astype(jnp.bfloat16)
+
+    names = ("y", "alive", "signed", "from_a", "from_b")
+    live["residual"], scaled = kernel_call("begin", assemble, (vector, rounded), *[live.pop(name) if name[0] in "fy" else live[name] for name in names])
+
+    def precond_blocks(product, signed, residual):
         y = signed[...] * product[...]
-        return (y, dot(residual[...], y), *messages(0, y, None, None, None, None, ()))
-
-    y, gamma_part, *sent = kernel_call(
-        "precond_tiles", precond_tiles, (vector, column, tile, tile), times(scaled, pre), signed, residual, place
-    )
-    tiles = exchange_by_permutes(y, sent, place)
-
-    def aim(y, alive, signed, place, *tiles):
-        direction = alive[...] * (y[...] + from_permutes(tiles, place))
-        return direction, (signed[...] * direction).astype(jnp.bfloat16)
-
-    direction, scaled = kernel_call("aim", aim, (vector, rounded), y, alive, signed, place, *tiles)
-
-    live = dict(alive=alive, signed=signed, residual=residual, direction=direction, dual=dual, pre=pre)
+        parity = Parity(HERE)
+        return y, dot(residual[...], y), placed(cube_b(y, parity), parity)
+
+    live["y"], live["gamma_part"], sent = kernel_call(
+        "precond_blocks",
+        precond_blocks,
+        (vector, column, CUBE),
+        times(scaled, live["pre"]),
+        live["signed"],
+        live["residual"],
+    )
+    live = exchange_by_cubes(sent, live)
+    live["direction"], scaled = kernel_call("aim", assemble, (vector, rounded), *[live.pop(name) if name[0] in "fy" else live[name] for name in names])
 
     def image_blocks(product, signed, direction, gamma_part, place):
         y = signed[...] * product[...]
@@ -296,9 +401,9 @@
         image_blocks,
         (vector, first_blocks),
         times(scaled, live["dual"]),
-        signed,
-        direction,
-        gamma_part,
+        live["signed"],
+        live["direction"],
+        live.pop("gamma_part"),
         place,
     )
     got, live = exchange_by_gathers(y, sent, place, 2, live)

time: 182 us -> 170 us (0.934)
  blocking collectives: 120 us -> 161 us
  starting transfers between devices: 37.4 us -> 0 us
  waiting for transfers between devices: 14.3 us -> 0 us
  other arithmetic: 2.37 us -> 0 us
    all_to_all x0 -> x4, blocking collectives: none -> 57.4 us  [cube_swap(): lax.all_to_all(sent, AXES, 0, 0, axis_index_groups=cubes(kind), tiled=True)]
    ppermute x12 -> x0, starting transfers between devices: 37.4 us -> none  [the longest x2 15.6 us: permuted(): near = lax.ppermute(tiles[0], axis, [(i, i ^ 1) for i in range(count)])]
    all_to_all x9, blocking collectives: 120 us -> 104 us  [gathered(): got = lax.all_to_all(sent, axis, 0, 0, tiled=True)]
    ppermute x12 -> x0, waiting for transfers between devices: 14.3 us -> none  [the longest x4 10.7 us: permuted(): after = lax.ppermute(tiles[1], axis, [(i + 1, i) for i in range(count - 1)])]
    pallas_call x20 -> x18, Pallas kernels: 4.32 us -> 4.34 us  [kernel_call(): pl.pallas_call(kernel, name=name, in_specs=[pl.BlockSpec(memory_space=plt...]
  transfers between devices with their start and end apart: 12 -> 0, of which waited for: 6 -> 0; matrix products, arithmetic and copies ran while one was open for 1% -> 0% of each run, Pallas kernels for 0% -> 0%
where the time goes in v4:
time: 170 us
  blocking collectives  161 us (95%)
  Pallas kernels  4.34 us (3%)
  local copies, waits for them, and re-layouts  2.22 us (1%)
    all_to_all x9, blocking collectives, gathered(): got = lax.all_to_all(sent, axis, 0, 0, tiled=True)  104 us
    all_to_all x4, blocking collectives, cube_swap(): lax.all_to_all(sent, AXES, 0, 0, axis_index_groups=cubes(kind), tiled=True)  57.4 us
    pallas_call x18, Pallas kernels, kernel_call(): pl.pallas_call(kernel, name=name, in_specs=[pl.BlockSpec(memory_space=plt...  4.34 us

profile of v4, /device:TPU:1, one launch (start us, length us, event | category | flops | bytes accessed | tf_op | source)
XLA Modules:
  0.0 169.6 jit_solution(6511390234227060496)
XLA Ops:
  0.6 0.0 copy-start
  0.6 0.9 copy.13
  1.5 0.0 copy-start.1
  1.5 0.7 copy-done.1
  2.2 0.0 copy-start.2
  2.2 0.7 copy-done.2
  2.9 0.2 load_blocks.1
  3.1 0.0 copy-done
  3.1 18.3 %all_to_all.65.refs_1_.refs_4_ = f32[8,16,128]{2,1,0:T(8,128)S(1)} all-to-all(f32[8,16,128]{2,1,0:T(8,128)S(1)} %get-tuple-element.270), channel_id=1, replica_groups={{0,15,112,127,896,911,1008,1023},{2,1,114,113,898,897,1010,1009},{4,3,1..., dimensions={0} | all-to-all | bytes 131072 | tf_op jit(solution)/shard_map/all_to_all | solution.py:260
  21.4 0.2 cube_a.2
  21.6 0.0 copy-start.3
  21.7 20.5 %all_to_all.66.refs_3_ = f32[8,16,128]{2,1,0:T(8,128)S(1)} all-to-all(f32[8,16,128]{2,1,0:T(8,128)S(1)} %cube_a.2), channel_id=1, replica_groups={{0,1,16,17,128,129,144,145},{2,3,18,19,130,131,146,147},{4,5,20,21,132,..., dimensions={0} | all-to-all | bytes 131072 | tf_op jit(solution)/shard_map/all_to_all | solution.py:260
  42.2 0.2 begin.1
  42.4 0.3 fusion.refs_0_
  42.7 0.2 precond_blocks.1
  42.9 9.1 %all_to_all.67.refs_1_.refs_4_ = f32[8,16,128]{2,1,0:T(8,128)S(1)} all-to-all(f32[8,16,128]{2,1,0:T(8,128)S(1)} %get-tuple-element.301), channel_id=1, replica_groups={{0,15,112,127,896,911,1008,1023},{2,1,114,113,898,897,1010,1009},{4,3,1..., dimensions={0} | all-to-all | bytes 131072 | tf_op jit(solution)/shard_map/all_to_all | solution.py:260
  52.1 0.2 cube_a.3
  52.3 9.3 %all_to_all.68.refs_3_ = f32[8,16,128]{2,1,0:T(8,128)S(1)} all-to-all(f32[8,16,128]{2,1,0:T(8,128)S(1)} %cube_a.3), channel_id=1, replica_groups={{0,1,16,17,128,129,144,145},{2,3,18,19,130,131,146,147},{4,5,20,21,132,..., dimensions={0} | all-to-all | bytes 131072 | tf_op jit(solution)/shard_map/all_to_all | solution.py:260
  61.6 0.2 aim.1
  61.9 0.0 copy-done.3
  61.9 0.3 fusion.1.refs_0_
  62.2 0.2 image_blocks.1
  62.4 11.2 %all_to_all.69.refs_1_ = f32[8,16,128]{2,1,0:T(8,128)S(1)} all-to-all(f32[8,16,128]{2,1,0:T(8,128)S(1)} %get-tuple-element.339), channel_id=1, replica_groups=mesh['gx'=8,'gy'=8,'gz'=16] {'gx'}, dimensions={0} | all-to-all | bytes 131072 | tf_op jit(solution)/shard_map/all_to_all | solution.py:288
  73.6 0.2 second_sum.3
  73.7 10.7 %all_to_all.70.refs_2_ = f32[8,16,128]{2,1,0:T(8,128)S(1)} all-to-all(f32[8,16,128]{2,1,0:T(8,128)S(1)} %get-tuple-element.357), channel_id=1, replica_groups=mesh['gx'=8,'gy'=8,'gz'=16] {'gy'}, dimensions={0} | all-to-all | bytes 131072 | tf_op jit(solution)/shard_map/all_to_all | solution.py:288
  84.4 0.2 third_sum.3
  84.7 15.2 %all_to_all.71.refs_0_ = f32[16,16,128]{2,1,0:T(8,128)S(1)} all-to-all(f32[16,16,128]{2,1,0:T(8,128)S(1)} %get-tuple-element.377), channel_id=1, replica_groups=mesh['gx'=8,'gy'=8,'gz'=16] {'gz'}, dimensions={0} | all-to-all | bytes 262144 | tf_op jit(solution)/shard_map/all_to_all | solution.py:288
  99.9 0.2 first_step.1
  100.2 0.3 fusion.2.refs_0_
  100.4 0.2 smooth_blocks.1
  100.6 10.5 %all_to_all.72.refs_1_ = f32[8,16,128]{2,1,0:T(8,128)S(1)} all-to-all(f32[8,16,128]{2,1,0:T(8,128)S(1)} %get-tuple-element.403), channel_id=1, replica_groups=mesh['gx'=8,'gy'=8,'gz'=16] {'gx'}, dimensions={0} | all-to-all | bytes 131072 | tf_op jit(solution)/shard_map/all_to_all | solution.py:288
  111.1 0.2 second_sum.4
  111.3 9.6 %all_to_all.73.refs_2_ = f32[8,16,128]{2,1,0:T(8,128)S(1)} all-to-all(f32[8,16,128]{2,1,0:T(8,128)S(1)} %get-tuple-element.423), channel_id=1, replica_groups=mesh['gx'=8,'gy'=8,'gz'=16] {'gy'}, dimensions={0} | all-to-all | bytes 131072 | tf_op jit(solution)/shard_map/all_to_all | solution.py:288
  120.9 0.2 third_sum.4
  121.1 13.2 %all_to_all.74.refs_0_ = f32[16,16,128]{2,1,0:T(8,128)S(1)} all-to-all(f32[16,16,128]{2,1,0:T(8,128)S(1)} %get-tuple-element.445), channel_id=1, replica_groups=mesh['gx'=8,'gy'=8,'gz'=16] {'gz'}, dimensions={0} | all-to-all | bytes 262144 | tf_op jit(solution)/shard_map/all_to_all | solution.py:288
  134.4 0.2 turn.1
  134.5 0.3 fusion.3.refs_0_
  134.8 0.2 sum_blocks.1
  135.0 10.5 %all_to_all.75.refs_1_ = f32[8,16,128]{2,1,0:T(8,128)S(1)} all-to-all(f32[8,16,128]{2,1,0:T(8,128)S(1)} %get-tuple-element.472), channel_id=1, replica_groups=mesh['gx'=8,'gy'=8,'gz'=16] {'gx'}, dimensions={0} | all-to-all | bytes 131072 | tf_op jit(solution)/shard_map/all_to_all | solution.py:288
  145.5 0.2 second_sum.5
  145.7 9.6 %all_to_all.76.refs_2_ = f32[8,16,128]{2,1,0:T(8,128)S(1)} all-to-all(f32[8,16,128]{2,1,0:T(8,128)S(1)} %get-tuple-element.490), channel_id=1, replica_groups=mesh['gx'=8,'gy'=8,'gz'=16] {'gy'}, dimensions={0} | all-to-all | bytes 131072 | tf_op jit(solution)/shard_map/all_to_all | solution.py:288
  155.3 0.2 third_sum.5
  155.5 13.2 %all_to_all.77.refs_0_ = f32[16,16,128]{2,1,0:T(8,128)S(1)} all-to-all(f32[16,16,128]{2,1,0:T(8,128)S(1)} %get-tuple-element.510), channel_id=1, replica_groups=mesh['gx'=8,'gy'=8,'gz'=16] {'gz'}, dimensions={0} | all-to-all | bytes 262144 | tf_op jit(solution)/shard_map/all_to_all | solution.py:288
  168.7 0.9 advance.1
Async XLA Ops:
  0.6 2.5 %copy-start = (bf16[1,1,1,768,768]{4,3,2,1,0:T(8,128)(2,1)S(1)}, bf16[1,1,1,768,768]{4,3,2,1,0:T(8,128)(2,1)}, u32[]{:S(2)}) copy-start(bf16[1,1,1,768,768]{4,3,2,1,0:T(8,128)(2,1)} %param.7) | copy-start | bytes 3538948
  1.5 0.7 copy-start.1
  2.2 0.7 copy-start.2
  21.6 40.2 %copy-start.3 = (bf16[1,1,1,768,768]{4,3,2,1,0:T(8,128)(2,1)S(1)}, bf16[1,1,1,768,768]{4,3,2,1,0:T(8,128)(2,1)}, u32[]{:S(2)}) copy-start(bf16[1,1,1,768,768]{4,3,2,1,0:T(8,128)(2,1)} %param.6) | copy-start | bytes 3538948

commit v5 on v4

--- a/solution.py
+++ b/solution.py
@@ -109,6 +109,15 @@
 HERE = Here()
 
 
+def store_blocks(ref, parts):
+    for i, part in enumerate(parts):
+        at, part = part if isinstance(part, tuple) else (i, part)
+        if part is None or part.shape != ref.shape[1:]:
+            ref[at] = jnp.zeros(ref.shape[1:], ref.dtype)
+        if part is not None:
+            ref[at, : part.shape[0], : part.shape[1]] = part
+
+
 def kernel_call(name, body, shapes, *operands, last=False):
     arrays = [pltpu.with_memory_space_constraint(value, pltpu.VMEM) for value in operands if value is not HERE]
 
@@ -117,12 +126,7 @@
         results = body(*[HERE if value is HERE else next(given) for value in operands])
         for ref, result in zip(given, results):
             if isinstance(result, list):
-                for i, part in enumerate(result):
-                    at, part = part if isinstance(part, tuple) else (i, part)
-                    if part is None or part.shape != ref.shape[1:]:
-                        ref[at] = jnp.zeros(ref.shape[1:], ref.dtype)
-                    if part is not None:
-                        ref[at, : part.shape[0], : part.shape[1]] = part
+                store_blocks(ref, result)
             elif result.shape != ref.shape:
                 lines = result.shape[1] // 128
                 for i in range(lines):
@@ -334,6 +338,48 @@
     return beside(*pair_of(x_tiles), *pair_of(y_tiles), unpack(before), unpack(after)), sums
 
 
+def load_call(loads, counts, signs, shapes):
+    def kernel(loads_in, counts_in, signs_in, y, sent, alive, signed, lines, counts, signs, arrived):
+        copies = [
+            pltpu.make_async_copy(source, target, arrived.at[i])
+            for i, (source, target) in enumerate(((loads_in, lines), (counts_in, counts), (signs_in, signs)))
+        ]
+        for copy in copies:
+            copy.start()
+        copies[0].wait()
+        cases = y.shape[0]
+        folds = y.shape[1] // 128
+        values = jnp.concatenate([lines[pl.ds(i, cases, stride=folds), :] for i in range(folds)], axis=1)
+        y[...] = values
+        parity = Parity(HERE)
+        store_blocks(sent, placed(cube_b(values, parity), parity))
+        copies[1].wait()
+        position = lax.broadcasted_iota(jnp.int32, (1, FACE), 1)
+        alive[...] = jnp.concatenate(
+            [
+                (position[:, : CAPACITY[course]] < counts[:, course : course + 1]).astype(jnp.float32)
+                for course in range(len(DIRECTIONS))
+            ],
+            axis=1,
+        )
+        copies[2].wait()
+        signed[...] = signs[...].astype(jnp.float32) * alive[...]
+
+    return pl.pallas_call(
+        kernel,
+        name="load_blocks",
+        in_specs=[pl.BlockSpec(memory_space=pl.ANY) for _ in range(3)],
+        out_specs=[pl.BlockSpec(memory_space=pltpu.VMEM) for _ in shapes],
+        out_shape=[pltpu.VMEM(shape.shape, shape.dtype) for shape in shapes],
+        scratch_shapes=[
+            pltpu.VMEM(loads.shape, loads.dtype),
+            pltpu.VMEM(counts.shape, counts.dtype),
+            pltpu.VMEM(signs.shape, signs.dtype),
+            pltpu.SemaphoreType.DMA((3,)),
+        ],
+    )(loads, counts, signs)
+
+
 def per_device(loads, dual_ops, precond, counts, signs):
     place = HERE
     dual, pre = dual_ops[0, 0, 0], precond[0, 0, 0]
@@ -350,22 +396,11 @@
     def dot(left, right):
         return jnp.sum(left * right, axis=1, keepdims=True)
 
-    def load_blocks(loads, counts, signs):
-        position = lax.broadcasted_iota(jnp.int32, (1, FACE), 1)
-        alive = [
-            (position[:, : CAPACITY[course]] < counts[:, course : course + 1]).astype(jnp.float32)
-            for course in range(len(DIRECTIONS))
-        ]
-        alive = jnp.concatenate(alive, axis=1)
-        parity = Parity(HERE)
-        return alive, signs[...].astype(jnp.float32) * alive, placed(cube_b(loads[...], parity), parity)
-
     row = jax.ShapeDtypeStruct((1, loads.shape[1]), jnp.float32)
     live = dict(dual=dual, pre=pre)
-    live["alive"], live["signed"], sent = kernel_call(
-        "load_blocks", load_blocks, (row, row, CUBE), loads, counts[0, 0], signs[0, 0]
-    )
-    live["y"] = loads
+    live["y"], sent, live["alive"], live["signed"] = load_call(
+        loads.reshape(-1, 128), counts[0, 0], signs[0, 0], (vector, CUBE, row, row)
+    )
     live = exchange_by_cubes(sent, live)
 
     def assemble(y, alive, signed, from_a, from_b):

time: 170 us -> 169 us (level)
  local copies, waits for them, and re-layouts: 2.22 us -> 0.03 us
    unnamed x9 -> x4, local copies, waits for them, and re-layouts: 2.22 us -> 0.03 us
    pallas_call x18 -> x17, Pallas kernels: 4.34 us -> 4.13 us  [kernel_call(): pl.pallas_call(kernel, name=name, in_specs=[pl.BlockSpec(memory_space=plt...]
where the time goes in v5:
time: 169 us; the launch traced here: 168 us
  blocking collectives  161 us (95%)
  Pallas kernels  5.41 us (3%)
    all_to_all x9, blocking collectives, gathered(): got = lax.all_to_all(sent, axis, 0, 0, tiled=True)  104 us
    all_to_all x4, blocking collectives, cube_swap(): lax.all_to_all(sent, AXES, 0, 0, axis_index_groups=cubes(kind), tiled=True)  57.4 us
    pallas_call x17, Pallas kernels, kernel_call(): pl.pallas_call(kernel, name=name, in_specs=[pl.BlockSpec(memory_space=plt...  4.13 us

profile of v5, /device:TPU:1, one launch (start us, length us, event | category | flops | bytes accessed | tf_op | source)
XLA Modules:
  0.0 168.5 jit_solution(17412736271588536206)
XLA Ops:
  0.6 0.0 copy-start
  0.6 1.3 load_blocks.1
  1.9 0.0 copy-done
  2.0 18.3 %all_to_all.65.refs_1_.refs_4_ = f32[8,16,128]{2,1,0:T(8,128)S(1)} all-to-all(f32[8,16,128]{2,1,0:T(8,128)S(1)} %get-tuple-element.272), channel_id=1, replica_groups={{0,15,112,127,896,911,1008,1023},{2,1,114,113,898,897,1010,1009},{4,3,1..., dimensions={0} | all-to-all | bytes 131072 | tf_op jit(solution)/shard_map/all_to_all | solution.py:264
  20.3 0.2 cube_a.2
  20.5 0.0 copy-start.1
  20.5 20.5 %all_to_all.66.refs_3_ = f32[8,16,128]{2,1,0:T(8,128)S(1)} all-to-all(f32[8,16,128]{2,1,0:T(8,128)S(1)} %cube_a.2), channel_id=1, replica_groups={{0,1,16,17,128,129,144,145},{2,3,18,19,130,131,146,147},{4,5,20,21,132,..., dimensions={0} | all-to-all | bytes 131072 | tf_op jit(solution)/shard_map/all_to_all | solution.py:264
  41.1 0.2 begin.1
  41.3 0.3 fusion.refs_0_
  41.6 0.2 precond_blocks.1
  41.8 9.1 %all_to_all.67.refs_1_.refs_4_ = f32[8,16,128]{2,1,0:T(8,128)S(1)} all-to-all(f32[8,16,128]{2,1,0:T(8,128)S(1)} %get-tuple-element.303), channel_id=1, replica_groups={{0,15,112,127,896,911,1008,1023},{2,1,114,113,898,897,1010,1009},{4,3,1..., dimensions={0} | all-to-all | bytes 131072 | tf_op jit(solution)/shard_map/all_to_all | solution.py:264
  50.9 0.2 cube_a.3
  51.2 9.3 %all_to_all.68.refs_3_ = f32[8,16,128]{2,1,0:T(8,128)S(1)} all-to-all(f32[8,16,128]{2,1,0:T(8,128)S(1)} %cube_a.3), channel_id=1, replica_groups={{0,1,16,17,128,129,144,145},{2,3,18,19,130,131,146,147},{4,5,20,21,132,..., dimensions={0} | all-to-all | bytes 131072 | tf_op jit(solution)/shard_map/all_to_all | solution.py:264
  60.5 0.2 aim.1
  60.7 0.0 copy-done.1
  60.7 0.3 fusion.1.refs_0_
  61.0 0.2 image_blocks.1
  61.2 11.2 %all_to_all.69.refs_1_ = f32[8,16,128]{2,1,0:T(8,128)S(1)} all-to-all(f32[8,16,128]{2,1,0:T(8,128)S(1)} %get-tuple-element.341), channel_id=1, replica_groups=mesh['gx'=8,'gy'=8,'gz'=16] {'gx'}, dimensions={0} | all-to-all | bytes 131072 | tf_op jit(solution)/shard_map/all_to_all | solution.py:292
  72.4 0.2 second_sum.3
  72.6 10.7 %all_to_all.70.refs_2_ = f32[8,16,128]{2,1,0:T(8,128)S(1)} all-to-all(f32[8,16,128]{2,1,0:T(8,128)S(1)} %get-tuple-element.359), channel_id=1, replica_groups=mesh['gx'=8,'gy'=8,'gz'=16] {'gy'}, dimensions={0} | all-to-all | bytes 131072 | tf_op jit(solution)/shard_map/all_to_all | solution.py:292
  83.3 0.2 third_sum.3
  83.5 15.2 %all_to_all.71.refs_0_ = f32[16,16,128]{2,1,0:T(8,128)S(1)} all-to-all(f32[16,16,128]{2,1,0:T(8,128)S(1)} %get-tuple-element.379), channel_id=1, replica_groups=mesh['gx'=8,'gy'=8,'gz'=16] {'gz'}, dimensions={0} | all-to-all | bytes 262144 | tf_op jit(solution)/shard_map/all_to_all | solution.py:292
  98.8 0.2 first_step.1
  99.0 0.3 fusion.2.refs_0_
  99.3 0.2 smooth_blocks.1
  99.5 10.5 %all_to_all.72.refs_1_ = f32[8,16,128]{2,1,0:T(8,128)S(1)} all-to-all(f32[8,16,128]{2,1,0:T(8,128)S(1)} %get-tuple-element.405), channel_id=1, replica_groups=mesh['gx'=8,'gy'=8,'gz'=16] {'gx'}, dimensions={0} | all-to-all | bytes 131072 | tf_op jit(solution)/shard_map/all_to_all | solution.py:292
  110.0 0.2 second_sum.4
  110.2 9.6 %all_to_all.73.refs_2_ = f32[8,16,128]{2,1,0:T(8,128)S(1)} all-to-all(f32[8,16,128]{2,1,0:T(8,128)S(1)} %get-tuple-element.425), channel_id=1, replica_groups=mesh['gx'=8,'gy'=8,'gz'=16] {'gy'}, dimensions={0} | all-to-all | bytes 131072 | tf_op jit(solution)/shard_map/all_to_all | solution.py:292
  119.7 0.2 third_sum.4
  120.0 13.2 %all_to_all.74.refs_0_ = f32[16,16,128]{2,1,0:T(8,128)S(1)} all-to-all(f32[16,16,128]{2,1,0:T(8,128)S(1)} %get-tuple-element.447), channel_id=1, replica_groups=mesh['gx'=8,'gy'=8,'gz'=16] {'gz'}, dimensions={0} | all-to-all | bytes 262144 | tf_op jit(solution)/shard_map/all_to_all | solution.py:292
  133.2 0.2 turn.1
  133.4 0.3 fusion.3.refs_0_
  133.7 0.2 sum_blocks.1
  133.9 10.5 %all_to_all.75.refs_1_ = f32[8,16,128]{2,1,0:T(8,128)S(1)} all-to-all(f32[8,16,128]{2,1,0:T(8,128)S(1)} %get-tuple-element.474), channel_id=1, replica_groups=mesh['gx'=8,'gy'=8,'gz'=16] {'gx'}, dimensions={0} | all-to-all | bytes 131072 | tf_op jit(solution)/shard_map/all_to_all | solution.py:292
  144.4 0.2 second_sum.5
  144.5 9.6 %all_to_all.76.refs_2_ = f32[8,16,128]{2,1,0:T(8,128)S(1)} all-to-all(f32[8,16,128]{2,1,0:T(8,128)S(1)} %get-tuple-element.492), channel_id=1, replica_groups=mesh['gx'=8,'gy'=8,'gz'=16] {'gy'}, dimensions={0} | all-to-all | bytes 131072 | tf_op jit(solution)/shard_map/all_to_all | solution.py:292
  154.1 0.2 third_sum.5
  154.4 13.2 %all_to_all.77.refs_0_ = f32[16,16,128]{2,1,0:T(8,128)S(1)} all-to-all(f32[16,16,128]{2,1,0:T(8,128)S(1)} %get-tuple-element.512), channel_id=1, replica_groups=mesh['gx'=8,'gy'=8,'gz'=16] {'gz'}, dimensions={0} | all-to-all | bytes 262144 | tf_op jit(solution)/shard_map/all_to_all | solution.py:292
  167.6 0.9 advance.1
Async XLA Ops:
  0.6 1.3 copy-start
  20.5 40.2 %copy-start.1 = (bf16[1,1,1,768,768]{4,3,2,1,0:T(8,128)(2,1)S(1)}, bf16[1,1,1,768,768]{4,3,2,1,0:T(8,128)(2,1)}, u32[]{:S(2)}) copy-start(bf16[1,1,1,768,768]{4,3,2,1,0:T(8,128)(2,1)} %param.6) | copy-start | bytes 3538948

commit v6 on v5

--- a/solution.py
+++ b/solution.py
@@ -91,10 +91,32 @@
     pieces = [
         px[0], mx[0], py[0], my[0], pz[0], mz[0],
         py[2], my[2], py[1], my[1],
+        pz[4], mz[4], pz[3], mz[3],
         pz[2], mz[2], pz[1], mz[1],
-        pz[4], mz[4], pz[3], mz[3],
     ]
     return jnp.concatenate(pieces, axis=1)
+
+
+def turned(values):
+    swapped = jnp.concatenate([block(values, y, x, z) for x, y, z in DIRECTIONS], axis=1)
+    return jnp.where(lax.rem(HERE[2], 2) == 0, values, swapped)
+
+
+def line_place(stage):
+    if stage == 2:
+        return HERE[2]
+    return jnp.where(lax.rem(HERE[2], 2) == 0, HERE[stage], HERE[1 - stage])
+
+
+def lines_of(stage):
+    sizes = [lax.axis_size(axis) for axis in AXES]
+    assert sizes[0] == sizes[1]
+    groups = []
+    for z in range(sizes[2]):
+        for fixed in range(sizes[0]):
+            places = [(i, fixed, z) if (stage + z) % 2 == 0 else (fixed, i, z) for i in range(sizes[0])]
+            groups.append([int(np.ravel_multi_index(place, sizes)) for place in places])
+    return groups
 
 
 AXES = ("gx", "gy", "gz")
@@ -289,13 +311,16 @@
 
 def gathered(stage, axis, sent, live):
     sent, live = lax.optimization_barrier((sent, live))
-    got = lax.all_to_all(sent, axis, 0, 0, tiled=True)
+    if stage < 2:
+        got = lax.all_to_all(sent, AXES, 0, 0, axis_index_groups=lines_of(stage), tiled=True)
+    else:
+        got = lax.all_to_all(sent, axis, 0, 0, tiled=True)
     return lax.optimization_barrier((got, live))
 
 
 def picked(got, place, stage, number):
     count = got.shape[0]
-    here = place[stage]
+    here = line_place(stage)
     before = got[jnp.maximum(here - 1, 0)]
     after = got[jnp.minimum(here + 1, count - 1)]
     low = got[0, 12:16, :]
@@ -317,7 +342,7 @@
     def second(y, got, place):
         before, after, sums = picked(got, place, 0, number)
         ahead, behind = messages(1, y[...], unpack(before), unpack(after), None, None, sums)
-        return spread(ahead, behind, place[1], sizes[1]), [before, after]
+        return spread(ahead, behind, line_place(1), sizes[1]), [before, after]
 
     sent, x_tiles = kernel_call("second_sum", second, (blocks(1), TILE), live["y"], got, HERE)
     live["x_tiles"] = x_tiles
@@ -326,7 +351,7 @@
     def third(y, x_tiles, got, place):
         before, after, sums = picked(got, place, 1, number)
         ahead, behind = messages(2, y[...], *pair_of(x_tiles), unpack(before), unpack(after), sums)
-        return spread(ahead, behind, place[2], sizes[2]), [before, after]
+        return spread(ahead, behind, line_place(2), sizes[2]), [before, after]
 
     sent, y_tiles = kernel_call("third_sum", third, (blocks(2), TILE), live["y"], live["x_tiles"], got, HERE)
     live["y_tiles"] = y_tiles
@@ -429,7 +454,8 @@
     def image_blocks(product, signed, direction, gamma_part, place):
         y = signed[...] * product[...]
         sums = (gamma_part[...], dot(direction[...], y))
-        return y, spread(*messages(0, y, None, None, None, None, sums), place[0], sizes[0])
+        y = turned(y)
+        return y, spread(*messages(0, y, None, None, None, None, sums), line_place(0), sizes[0])
 
     y, sent = kernel_call(
         "image_blocks",
@@ -445,7 +471,7 @@
 
     def first_step(got, x_tiles, y_tiles, y, place, alive, signed, direction, residual):
         near, (gamma, curvature) = from_gathers(got, x_tiles, y_tiles, place, 2)
-        image = alive[...] * (y[...] + near)
+        image = alive[...] * turned(y[...] + near)
         step = gamma / curvature
         left = residual[...] - step * image
         return step * direction[...], left, (signed[...] * left).astype(jnp.bfloat16), gamma
@@ -458,7 +484,8 @@
     def sum_blocks(product, signed, left, place):
         y = signed[...] * product[...]
         sums = (dot(left[...], y),)
-        return y, spread(*messages(0, y, None, None, None, None, sums), place[0], sizes[0])
+        y = turned(y)
+        return y, spread(*messages(0, y, None, None, None, None, sums), line_place(0), sizes[0])
 
     for iteration in range(1, ITERS):
         y, sent = kernel_call(
@@ -474,9 +501,9 @@
 
         def turn(got, x_tiles, y_tiles, y, place, alive, signed, direction, gamma_old):
             near, (gamma,) = from_gathers(got, x_tiles, y_tiles, place, 1)
-            smoothed = alive[...] * (y[...] + near)
-            turned = smoothed + (gamma / gamma_old[...]) * direction[...]
-            return turned, (signed[...] * turned).astype(jnp.bfloat16), gamma
+            smoothed = alive[...] * turned(y[...] + near)
+            fresh = smoothed + (gamma / gamma_old[...]) * direction[...]
+            return fresh, (signed[...] * fresh).astype(jnp.bfloat16), gamma
 
         names = ("x_tiles", "y_tiles", "y", "place", "alive", "signed", "direction", "gamma")
         live["direction"], scaled, live["gamma"] = kernel_call(
@@ -495,7 +522,7 @@
 
         def advance(got, x_tiles, y_tiles, y, place, alive, signed, direction, gamma, multipliers, residual):
             near, (curvature,) = from_gathers(got, x_tiles, y_tiles, place, 1)
-            image = alive[...] * (y[...] + near)
+            image = alive[...] * turned(y[...] + near)
             step = gamma[...] / curvature
             left = residual[...] - step * image
             results = (multipliers[...] + step * direction[...], left)

time: 169 us -> 169 us (level)
    all_to_all x9 -> x3, blocking collectives: 104 us -> 42.7 us  [gathered(): got = lax.all_to_all(sent, axis, 0, 0, tiled=True)]
    all_to_all x0 -> x6, blocking collectives: none -> 60.3 us  [gathered(): lax.all_to_all(sent, AXES, 0, 0, axis_index_groups=lines_of(stage), tiled...]
where the time goes in v6:
time: 169 us; the launch traced here: 168 us
  blocking collectives  160 us (95%)
  Pallas kernels  5.6 us (3%)
    all_to_all x6, blocking collectives, gathered(): lax.all_to_all(sent, AXES, 0, 0, axis_index_groups=lines_of(stage), tiled...  60.3 us
    all_to_all x4, blocking collectives, cube_swap(): lax.all_to_all(sent, AXES, 0, 0, axis_index_groups=cubes(kind), tiled=True)  57.4 us
    all_to_all x3, blocking collectives, gathered(): got = lax.all_to_all(sent, axis, 0, 0, tiled=True)  42.7 us
    pallas_call x17, Pallas kernels, kernel_call(): pl.pallas_call(kernel, name=name, in_specs=[pl.BlockSpec(memory_space=plt...  4.32 us

profile of v6, /device:TPU:1, one launch (start us, length us, event | category | flops | bytes accessed | tf_op | source)
XLA Modules:
  0.0 167.9 jit_solution(10972557538922752177)
XLA Ops:
  0.6 0.0 copy-start
  0.6 1.3 load_blocks.1
  1.9 0.0 copy-done
  2.0 18.3 %all_to_all.65.refs_1_.refs_4_ = f32[8,16,128]{2,1,0:T(8,128)S(1)} all-to-all(f32[8,16,128]{2,1,0:T(8,128)S(1)} %get-tuple-element.272), channel_id=1, replica_groups={{0,15,112,127,896,911,1008,1023},{2,1,114,113,898,897,1010,1009},{4,3,1..., dimensions={0} | all-to-all | bytes 131072 | tf_op jit(solution)/shard_map/all_to_all | solution.py:286
  20.3 0.2 cube_a.2
  20.5 0.0 copy-start.1
  20.5 20.5 %all_to_all.66.refs_3_ = f32[8,16,128]{2,1,0:T(8,128)S(1)} all-to-all(f32[8,16,128]{2,1,0:T(8,128)S(1)} %cube_a.2), channel_id=1, replica_groups={{0,1,16,17,128,129,144,145},{2,3,18,19,130,131,146,147},{4,5,20,21,132,..., dimensions={0} | all-to-all | bytes 131072 | tf_op jit(solution)/shard_map/all_to_all | solution.py:286
  41.1 0.2 begin.1
  41.3 0.3 fusion.refs_0_
  41.6 0.2 precond_blocks.1
  41.8 9.1 %all_to_all.67.refs_1_.refs_4_ = f32[8,16,128]{2,1,0:T(8,128)S(1)} all-to-all(f32[8,16,128]{2,1,0:T(8,128)S(1)} %get-tuple-element.303), channel_id=1, replica_groups={{0,15,112,127,896,911,1008,1023},{2,1,114,113,898,897,1010,1009},{4,3,1..., dimensions={0} | all-to-all | bytes 131072 | tf_op jit(solution)/shard_map/all_to_all | solution.py:286
  50.9 0.2 cube_a.3
  51.2 9.3 %all_to_all.68.refs_3_ = f32[8,16,128]{2,1,0:T(8,128)S(1)} all-to-all(f32[8,16,128]{2,1,0:T(8,128)S(1)} %cube_a.3), channel_id=1, replica_groups={{0,1,16,17,128,129,144,145},{2,3,18,19,130,131,146,147},{4,5,20,21,132,..., dimensions={0} | all-to-all | bytes 131072 | tf_op jit(solution)/shard_map/all_to_all | solution.py:286
  60.5 0.2 aim.1
  60.7 0.0 copy-done.1
  60.7 0.3 fusion.1.refs_0_
  61.0 0.2 image_blocks.1
  61.3 10.6 %all_to_all.69.refs_1_ = f32[8,16,128]{2,1,0:T(8,128)S(1)} all-to-all(f32[8,16,128]{2,1,0:T(8,128)S(1)} %get-tuple-element.341), channel_id=1, replica_groups={{0,128,256,384,512,640,768,896},{16,144,272,400,528,656,784,912},{32,16..., dimensions={0} | all-to-all | bytes 131072 | tf_op jit(solution)/shard_map/all_to_all | solution.py:315
  71.9 0.2 second_sum.3
  72.0 11.3 %all_to_all.70.refs_2_ = f32[8,16,128]{2,1,0:T(8,128)S(1)} all-to-all(f32[8,16,128]{2,1,0:T(8,128)S(1)} %get-tuple-element.359), channel_id=1, replica_groups={{0,16,32,48,64,80,96,112},{128,144,160,176,192,208,224,240},{256,272,28..., dimensions={0} | all-to-all | bytes 131072 | tf_op jit(solution)/shard_map/all_to_all | solution.py:315
  83.3 0.2 third_sum.3
  83.6 15.2 %all_to_all.71.refs_0_ = f32[16,16,128]{2,1,0:T(8,128)S(1)} all-to-all(f32[16,16,128]{2,1,0:T(8,128)S(1)} %get-tuple-element.379), channel_id=1, replica_groups=mesh['gx'=8,'gy'=8,'gz'=16] {'gz'}, dimensions={0} | all-to-all | bytes 262144 | tf_op jit(solution)/shard_map/all_to_all | solution.py:317
  98.8 0.2 first_step.1
  99.1 0.3 fusion.2.refs_0_
  99.3 0.2 smooth_blocks.1
  99.6 9.6 %all_to_all.72.refs_1_ = f32[8,16,128]{2,1,0:T(8,128)S(1)} all-to-all(f32[8,16,128]{2,1,0:T(8,128)S(1)} %get-tuple-element.405), channel_id=1, replica_groups={{0,128,256,384,512,640,768,896},{16,144,272,400,528,656,784,912},{32,16..., dimensions={0} | all-to-all | bytes 131072 | tf_op jit(solution)/shard_map/all_to_all | solution.py:315
  109.2 0.2 second_sum.4
  109.3 9.6 %all_to_all.73.refs_2_ = f32[8,16,128]{2,1,0:T(8,128)S(1)} all-to-all(f32[8,16,128]{2,1,0:T(8,128)S(1)} %get-tuple-element.425), channel_id=1, replica_groups={{0,16,32,48,64,80,96,112},{128,144,160,176,192,208,224,240},{256,272,28..., dimensions={0} | all-to-all | bytes 131072 | tf_op jit(solution)/shard_map/all_to_all | solution.py:315
  118.9 0.2 third_sum.4
  119.2 13.6 %all_to_all.74.refs_0_ = f32[16,16,128]{2,1,0:T(8,128)S(1)} all-to-all(f32[16,16,128]{2,1,0:T(8,128)S(1)} %get-tuple-element.447), channel_id=1, replica_groups=mesh['gx'=8,'gy'=8,'gz'=16] {'gz'}, dimensions={0} | all-to-all | bytes 262144 | tf_op jit(solution)/shard_map/all_to_all | solution.py:317
  132.8 0.2 turn.1
  133.0 0.3 fusion.3.refs_0_
  133.3 0.2 sum_blocks.1
  133.5 9.6 %all_to_all.75.refs_1_ = f32[8,16,128]{2,1,0:T(8,128)S(1)} all-to-all(f32[8,16,128]{2,1,0:T(8,128)S(1)} %get-tuple-element.474), channel_id=1, replica_groups={{0,128,256,384,512,640,768,896},{16,144,272,400,528,656,784,912},{32,16..., dimensions={0} | all-to-all | bytes 131072 | tf_op jit(solution)/shard_map/all_to_all | solution.py:315
  143.1 0.2 second_sum.5
  143.3 9.6 %all_to_all.76.refs_2_ = f32[8,16,128]{2,1,0:T(8,128)S(1)} all-to-all(f32[8,16,128]{2,1,0:T(8,128)S(1)} %get-tuple-element.492), channel_id=1, replica_groups={{0,16,32,48,64,80,96,112},{128,144,160,176,192,208,224,240},{256,272,28..., dimensions={0} | all-to-all | bytes 131072 | tf_op jit(solution)/shard_map/all_to_all | solution.py:315
  152.9 0.2 third_sum.5
  153.2 13.9 %all_to_all.77.refs_0_ = f32[16,16,128]{2,1,0:T(8,128)S(1)} all-to-all(f32[16,16,128]{2,1,0:T(8,128)S(1)} %get-tuple-element.512), channel_id=1, replica_groups=mesh['gx'=8,'gy'=8,'gz'=16] {'gz'}, dimensions={0} | all-to-all | bytes 262144 | tf_op jit(solution)/shard_map/all_to_all | solution.py:317
  167.0 0.9 advance.1
Async XLA Ops:
  0.6 1.3 copy-start
  20.5 40.2 %copy-start.1 = (bf16[1,1,1,768,768]{4,3,2,1,0:T(8,128)(2,1)S(1)}, bf16[1,1,1,768,768]{4,3,2,1,0:T(8,128)(2,1)}, u32[]{:S(2)}) copy-start(bf16[1,1,1,768,768]{4,3,2,1,0:T(8,128)(2,1)} %param.6) | copy-start | bytes 3538948

commit v7 on v6

--- a/solution.py
+++ b/solution.py
@@ -156,12 +156,35 @@
             else:
                 ref[...] = result
 
+    if last:
+
+        def leaving(*refs):
+            count = len(arrays)
+            given, left, kept, sent = refs[:count], refs[count:-len(shapes) - 1], refs[-len(shapes) - 1 : -1], refs[-1]
+            kernel(*given, *kept)
+            copies = [pltpu.make_async_copy(*pair, sent.at[i]) for i, pair in enumerate(zip(kept, left))]
+            for copy in copies:
+                copy.start()
+            for copy in copies:
+                copy.wait()
+
+        return pl.pallas_call(
+            leaving,
+            name=name,
+            in_specs=[pl.BlockSpec(memory_space=pltpu.VMEM) for _ in arrays],
+            out_specs=[pl.BlockSpec(memory_space=pl.ANY) for _ in shapes],
+            out_shape=list(shapes),
+            scratch_shapes=[
+                *[pltpu.VMEM(shape.shape, shape.dtype) for shape in shapes],
+                pltpu.SemaphoreType.DMA((len(shapes),)),
+            ],
+        )(*arrays)
     return pl.pallas_call(
         kernel,
         name=name,
         in_specs=[pl.BlockSpec(memory_space=pltpu.VMEM) for _ in arrays],
         out_specs=[pl.BlockSpec(memory_space=pltpu.VMEM) for _ in shapes],
-        out_shape=[shape if last else pltpu.VMEM(shape.shape, shape.dtype) for shape in shapes],
+        out_shape=[pltpu.VMEM(shape.shape, shape.dtype) for shape in shapes],
     )(*arrays)
 
 

time: 169 us -> 169 us (level)
    pallas_call x17 -> x16, Pallas kernels: 4.32 us -> 3.44 us  [kernel_call(): pl.pallas_call(kernel, name=name, in_specs=[pl.BlockSpec(memory_space=plt...]
where the time goes in v7:
time: 169 us; the launch traced here: 168 us
  blocking collectives  160 us (95%)
  Pallas kernels  5.62 us (3%)
    all_to_all x6, blocking collectives, gathered(): lax.all_to_all(sent, AXES, 0, 0, axis_index_groups=lines_of(stage), tiled...  60.3 us
    all_to_all x4, blocking collectives, cube_swap(): lax.all_to_all(sent, AXES, 0, 0, axis_index_groups=cubes(kind), tiled=True)  57.4 us
    all_to_all x3, blocking collectives, gathered(): got = lax.all_to_all(sent, axis, 0, 0, tiled=True)  42.7 us
    pallas_call x16, Pallas kernels, kernel_call(): pl.pallas_call(kernel, name=name, in_specs=[pl.BlockSpec(memory_space=plt...  3.44 us

profile of v7, /device:TPU:1, one launch (start us, length us, event | category | flops | bytes accessed | tf_op | source)
XLA Modules:
  0.0 167.9 jit_solution(4290982290927135690)
XLA Ops:
  0.6 0.0 copy-start
  0.6 1.3 load_blocks.1
  1.9 0.0 copy-done
  2.0 18.3 %all_to_all.65.refs_1_.refs_4_ = f32[8,16,128]{2,1,0:T(8,128)S(1)} all-to-all(f32[8,16,128]{2,1,0:T(8,128)S(1)} %get-tuple-element.272), channel_id=1, replica_groups={{0,15,112,127,896,911,1008,1023},{2,1,114,113,898,897,1010,1009},{4,3,1..., dimensions={0} | all-to-all | bytes 131072 | tf_op jit(solution)/shard_map/all_to_all | solution.py:309
  20.3 0.2 cube_a.2
  20.5 0.0 copy-start.1
  20.5 20.5 %all_to_all.66.refs_3_ = f32[8,16,128]{2,1,0:T(8,128)S(1)} all-to-all(f32[8,16,128]{2,1,0:T(8,128)S(1)} %cube_a.2), channel_id=1, replica_groups={{0,1,16,17,128,129,144,145},{2,3,18,19,130,131,146,147},{4,5,20,21,132,..., dimensions={0} | all-to-all | bytes 131072 | tf_op jit(solution)/shard_map/all_to_all | solution.py:309
  41.1 0.2 begin.1
  41.3 0.3 fusion.refs_0_
  41.6 0.2 precond_blocks.1
  41.8 9.1 %all_to_all.67.refs_1_.refs_4_ = f32[8,16,128]{2,1,0:T(8,128)S(1)} all-to-all(f32[8,16,128]{2,1,0:T(8,128)S(1)} %get-tuple-element.303), channel_id=1, replica_groups={{0,15,112,127,896,911,1008,1023},{2,1,114,113,898,897,1010,1009},{4,3,1..., dimensions={0} | all-to-all | bytes 131072 | tf_op jit(solution)/shard_map/all_to_all | solution.py:309
  50.9 0.2 cube_a.3
  51.2 9.3 %all_to_all.68.refs_3_ = f32[8,16,128]{2,1,0:T(8,128)S(1)} all-to-all(f32[8,16,128]{2,1,0:T(8,128)S(1)} %cube_a.3), channel_id=1, replica_groups={{0,1,16,17,128,129,144,145},{2,3,18,19,130,131,146,147},{4,5,20,21,132,..., dimensions={0} | all-to-all | bytes 131072 | tf_op jit(solution)/shard_map/all_to_all | solution.py:309
  60.5 0.2 aim.1
  60.7 0.0 copy-done.1
  60.7 0.3 fusion.1.refs_0_
  61.0 0.2 image_blocks.1
  61.3 10.6 %all_to_all.69.refs_1_ = f32[8,16,128]{2,1,0:T(8,128)S(1)} all-to-all(f32[8,16,128]{2,1,0:T(8,128)S(1)} %get-tuple-element.341), channel_id=1, replica_groups={{0,128,256,384,512,640,768,896},{16,144,272,400,528,656,784,912},{32,16..., dimensions={0} | all-to-all | bytes 131072 | tf_op jit(solution)/shard_map/all_to_all | solution.py:338
  71.9 0.2 second_sum.3
  72.0 11.3 %all_to_all.70.refs_2_ = f32[8,16,128]{2,1,0:T(8,128)S(1)} all-to-all(f32[8,16,128]{2,1,0:T(8,128)S(1)} %get-tuple-element.359), channel_id=1, replica_groups={{0,16,32,48,64,80,96,112},{128,144,160,176,192,208,224,240},{256,272,28..., dimensions={0} | all-to-all | bytes 131072 | tf_op jit(solution)/shard_map/all_to_all | solution.py:338
  83.3 0.2 third_sum.3
  83.6 15.2 %all_to_all.71.refs_0_ = f32[16,16,128]{2,1,0:T(8,128)S(1)} all-to-all(f32[16,16,128]{2,1,0:T(8,128)S(1)} %get-tuple-element.379), channel_id=1, replica_groups=mesh['gx'=8,'gy'=8,'gz'=16] {'gz'}, dimensions={0} | all-to-all | bytes 262144 | tf_op jit(solution)/shard_map/all_to_all | solution.py:340
  98.8 0.2 first_step.1
  99.1 0.3 fusion.2.refs_0_
  99.3 0.2 smooth_blocks.1
  99.6 9.6 %all_to_all.72.refs_1_ = f32[8,16,128]{2,1,0:T(8,128)S(1)} all-to-all(f32[8,16,128]{2,1,0:T(8,128)S(1)} %get-tuple-element.405), channel_id=1, replica_groups={{0,128,256,384,512,640,768,896},{16,144,272,400,528,656,784,912},{32,16..., dimensions={0} | all-to-all | bytes 131072 | tf_op jit(solution)/shard_map/all_to_all | solution.py:338
  109.2 0.2 second_sum.4
  109.3 9.6 %all_to_all.73.refs_2_ = f32[8,16,128]{2,1,0:T(8,128)S(1)} all-to-all(f32[8,16,128]{2,1,0:T(8,128)S(1)} %get-tuple-element.425), channel_id=1, replica_groups={{0,16,32,48,64,80,96,112},{128,144,160,176,192,208,224,240},{256,272,28..., dimensions={0} | all-to-all | bytes 131072 | tf_op jit(solution)/shard_map/all_to_all | solution.py:338
  118.9 0.2 third_sum.4
  119.2 13.6 %all_to_all.74.refs_0_ = f32[16,16,128]{2,1,0:T(8,128)S(1)} all-to-all(f32[16,16,128]{2,1,0:T(8,128)S(1)} %get-tuple-element.447), channel_id=1, replica_groups=mesh['gx'=8,'gy'=8,'gz'=16] {'gz'}, dimensions={0} | all-to-all | bytes 262144 | tf_op jit(solution)/shard_map/all_to_all | solution.py:340
  132.8 0.2 turn.1
  133.0 0.3 fusion.3.refs_0_
  133.3 0.2 sum_blocks.1
  133.5 9.6 %all_to_all.75.refs_1_ = f32[8,16,128]{2,1,0:T(8,128)S(1)} all-to-all(f32[8,16,128]{2,1,0:T(8,128)S(1)} %get-tuple-element.474), channel_id=1, replica_groups={{0,128,256,384,512,640,768,896},{16,144,272,400,528,656,784,912},{32,16..., dimensions={0} | all-to-all | bytes 131072 | tf_op jit(solution)/shard_map/all_to_all | solution.py:338
  143.1 0.2 second_sum.5
  143.3 9.6 %all_to_all.76.refs_2_ = f32[8,16,128]{2,1,0:T(8,128)S(1)} all-to-all(f32[8,16,128]{2,1,0:T(8,128)S(1)} %get-tuple-element.492), channel_id=1, replica_groups={{0,16,32,48,64,80,96,112},{128,144,160,176,192,208,224,240},{256,272,28..., dimensions={0} | all-to-all | bytes 131072 | tf_op jit(solution)/shard_map/all_to_all | solution.py:338
  152.9 0.2 third_sum.5
  153.2 13.9 %all_to_all.77.refs_0_ = f32[16,16,128]{2,1,0:T(8,128)S(1)} all-to-all(f32[16,16,128]{2,1,0:T(8,128)S(1)} %get-tuple-element.512), channel_id=1, replica_groups=mesh['gx'=8,'gy'=8,'gz'=16] {'gz'}, dimensions={0} | all-to-all | bytes 262144 | tf_op jit(solution)/shard_map/all_to_all | solution.py:340
  167.0 0.9 advance.1
Async XLA Ops:
  0.6 1.3 copy-start
  20.5 40.2 %copy-start.1 = (bf16[1,1,1,768,768]{4,3,2,1,0:T(8,128)(2,1)S(1)}, bf16[1,1,1,768,768]{4,3,2,1,0:T(8,128)(2,1)}, u32[]{:S(2)}) copy-start(bf16[1,1,1,768,768]{4,3,2,1,0:T(8,128)(2,1)} %param.6) | copy-start | bytes 3538948
